TPU v7x, 32 devices: a whole 2x2x4 slice. The times are simulated.
32 devices in a mesh: groups: 2 (over x), blocks: 16 (over z, y, core).
Axes of the slice: x: 2, y: 2, z: 4, core: 2. Of those that a mesh axis runs over, the one named last changes fastest.
Arguments:
- estimate: float32 [512, 128, 128], P(('groups', 'blocks')), parts along dimension 0, may hold values from 0.5 to 1.5
- images: bfloat16 [8, 512, 128, 128], P(None, ('groups', 'blocks')), parts along dimension 1, may hold values from 0.25 to 2
- point_spread: float32 [8, 3, 31], replicated, may hold values from 0.05 to 1
- shifts: int32 [8], replicated, may hold values from -32 to 32, as said below
Outputs:
- restored: float32 [512, 128, 128], P(('groups', 'blocks')), parts along dimension 0
There are 2 independent parts, one for each index of `groups`. A program takes and returns all parts, laid end to end along the dimension named above; an argument that names none is the same for every part. Nothing has to cross between parts.
Inputs may be any that keep to these rules, and one draw needn't show every extreme that they name: `shifts`: one view is placed at exactly 32 and another at exactly -32.
All inputs are finite; a program needn't handle non-finite values.
Results may differ from a plain program's by a relative error of at most 0.00031.
Values may be sent and summed in bfloat16 or wider, within the bound.
A program may use at most 128 MiB of HBM per device.

v0:
```python
import jax
import jax.numpy as jnp
from jax import lax
from jax.sharding import PartitionSpec as P


def passed_along(value, axis, steps):
    count = lax.axis_size(axis)
    initial, last = (max(0, -steps), min(count, count - steps))
    return lax.ppermute(value, axis, [(source, source + steps) for source in range(initial, last)])


def extended(block, sides, width):
    for axis, dim in sides:
        count = lax.axis_size(axis)
        forward = [(i, i + 1) for i in range(count - 1)]
        backward = [(target, source) for source, target in forward]
        low = lax.ppermute(
            lax.slice_in_dim(block, block.shape[dim] - width, None, axis=dim), axis, forward
        )
        high = lax.ppermute(lax.slice_in_dim(block, 0, width, axis=dim), axis, backward)
        block = jnp.concatenate([low, block, high], axis=dim)
    return block


def banded(tap_values, count_in, count_out, offset, direction):
    row_index = jnp.arange(count_in)[:, None]
    col_index = jnp.arange(count_out)[None, :]
    position = direction * (row_index - col_index) + offset
    matches = position[:, :, None] == jnp.arange(tap_values.shape[0])[None, None, :]
    spread = jnp.where(matches, tap_values.astype(jnp.float32)[None, None, :], jnp.float32(0.0))
    return jnp.sum(spread, axis=2).astype(jnp.bfloat16)


def forward(window, z_matrix, y_matrix, x_matrix):
    blur_z = jnp.einsum("wyz,zk->wyk", window, z_matrix, preferred_element_type=jnp.float32).astype(
        jnp.bfloat16
    )
    blur_y = jnp.einsum("wyz,yk->wkz", blur_z, y_matrix, preferred_element_type=jnp.float32).astype(
        jnp.bfloat16
    )
    return jnp.einsum("wyz,wi->iyz", blur_y, x_matrix, preferred_element_type=jnp.float32)


def adjoint(window, z_matrix, y_matrix, x_matrix):
    back_x = jnp.einsum("wyz,wi->iyz", window, x_matrix, preferred_element_type=jnp.float32).astype(
        jnp.bfloat16
    )
    back_y = jnp.einsum("xkz,yk->xyz", back_x, y_matrix, preferred_element_type=jnp.float32).astype(
        jnp.bfloat16
    )
    return jnp.einsum("xyk,zk->xyz", back_y, z_matrix, preferred_element_type=jnp.float32)


def image_rows(block):
    pieces = []
    for offset in range(-2, 3):
        if offset == 0:
            pieces.append(block)
        else:
            pieces.append(passed_along(block, "blocks", -offset))
    return jnp.concatenate(pieces, axis=0)


def body(estimate, images, point_spread, shifts):
    view_count = images.shape[0]
    slab_rows = estimate.shape[0]
    across = estimate.shape[1]
    along = estimate.shape[2]
    margin = point_spread.shape[2] // 2
    kernel = (point_spread / jnp.sum(point_spread, axis=2, keepdims=True)).astype(jnp.bfloat16)
    matrices = []
    for view in range(view_count):
        z_matrix = banded(kernel[view, 2], along, along, margin, 1)
        y_matrix = banded(kernel[view, 1], across, across, margin, 1)
        x_forward = banded(kernel[view, 0], slab_rows + 2 * margin, slab_rows, 0, 1)
        x_adjoint = banded(kernel[view, 0], slab_rows + 2 * margin, slab_rows, 2 * margin, -1)
        matrices.append((z_matrix, y_matrix, x_forward, x_adjoint))
    current = estimate
    aligned = []
    for view in range(view_count):
        window = image_rows(images[view])
        aligned.append(lax.dynamic_slice_in_dim(window, 2 * slab_rows + shifts[view], slab_rows, 0))
    padded = extended(current.astype(jnp.bfloat16), (("blocks", 0),), margin)
    quotients = []
    for view in range(view_count):
        z_matrix, y_matrix, x_forward, x_adjoint = matrices[view]
        predicted = forward(padded, z_matrix, y_matrix, x_forward)
        quotients.append((aligned[view].astype(jnp.float32) / predicted).astype(jnp.bfloat16))
    ratio_rims = extended(jnp.stack(quotients), (("blocks", 1),), margin)
    summed = jnp.zeros(estimate.shape, jnp.float32)
    for view in range(view_count):
        z_matrix, y_matrix, x_forward, x_adjoint = matrices[view]
        summed = summed + adjoint(ratio_rims[view], z_matrix, y_matrix, x_adjoint)
    current = current * summed / view_count
    return current


def solution(mesh):
    in_specs = (
        P(("groups", "blocks"), None, None),
        P(None, ("groups", "blocks"), None, None),
        P(),
        P(),
    )
    out_specs = P(("groups", "blocks"), None, None)
    return jax.shard_map(body, mesh=mesh, in_specs=in_specs, out_specs=out_specs, check_vma=False)
```

profile of v0, /device:TPU:22, one launch (start us, length us, event | category | flops | bytes accessed | tf_op | source)
XLA Modules:
  0.0 457.7 jit_solution(9192921167640452533)
XLA Ops:
  4.5 3.6 collective-permute-start.5
  12.0 4.3 collective-permute-start
  42.0 6.8 %select_reduce_fusion.1 = (bf16[128,128]{1,0:T(8,128)(2,1)S(1)}, bf16[128,128]{1,0:T(8,128)(2,1)S(1)}, bf16[128,128]{1,0:T(8,128)(2,1)S(1)}, bf16[128,128]{1,0:T...) fusion(f32[31]{0:T(128)} %get-tuple-element.59, ...), kind=kLoop, calls=%fused_computation.2 | loop fusion | flops 16498688 | bytes 591808 | tf_op jit(solution)/shard_map/reduce_sum | solution.py:32
  81.6 21.8 %collective-permute-start.22 = (bf16[16,128,128]{2,0,1:T(8,128)(2,1)}, bf16[16,128,128]{2,0,1:T(8,128)(2,1)S(1)}, u32[]{:S(2)}, u32[]{:S(2)}) collective-permute-start(bf16[16,128,128]{2,0,1:T(8,128)(2,1)} %bitcast.456), channel_id=1, source_target_pairs={{0,2},{1,3},{2,4},{3,5},{4,6},{5,7},{6,8},{7,9},{8,10},{9,11},{10,... | collective-permute-start | bytes 1572872 | tf_op jit(solution)/shard_map/ppermute | solution.py:10
  113.6 3.8 collective-permute-start.2
  118.4 4.8 %collective-permute-start.3 = (bf16[16,128,128]{2,0,1:T(8,128)(2,1)}, bf16[16,128,128]{2,0,1:T(8,128)(2,1)S(1)}, u32[]{:S(2)}, u32[]{:S(2)}) collective-permute-start(bf16[16,128,128]{2,0,1:T(8,128)(2,1)} %bitcast.447), channel_id=1, source_target_pairs={{2,0},{3,1},{4,2},{5,3},{6,4},{7,5},{8,6},{9,7},{10,8},{11,9},{12,... | collective-permute-start | bytes 1572872 | tf_op jit(solution)/shard_map/ppermute | solution.py:10
  123.3 15.0 %collective-permute-done.26 = bf16[16,128,128]{2,0,1:T(8,128)(2,1)S(1)} collective-permute-done((bf16[16,128,128]{2,0,1:T(8,128)(2,1)}, bf16[16,128,128]{2,0,1:T(8,128)(2,1)S(1)}, u32[]{:S(2)}, u32[]{:S(2)}) %collective-permute-start.26) | collective-permute-done | bytes 524320 | tf_op jit(solution)/shard_map/ppermute | solution.py:10
  138.3 5.1 %collective-permute-start.7 = (bf16[16,128,128]{2,0,1:T(8,128)(2,1)}, bf16[16,128,128]{2,0,1:T(8,128)(2,1)S(1)}, u32[]{:S(2)}, u32[]{:S(2)}) collective-permute-start(bf16[16,128,128]{2,0,1:T(8,128)(2,1)} %bitcast.446), channel_id=1, source_target_pairs={{0,1},{1,2},{2,3},{3,4},{4,5},{5,6},{6,7},{7,8},{8,9},{9,10},{10,1... | collective-permute-start | bytes 1572872 | tf_op jit(solution)/shard_map/ppermute | solution.py:10
  143.5 6.1 %collective-permute-done.30 = bf16[16,128,128]{2,0,1:T(8,128)(2,1)S(1)} collective-permute-done((bf16[16,128,128]{2,0,1:T(8,128)(2,1)}, bf16[16,128,128]{2,0,1:T(8,128)(2,1)S(1)}, u32[]{:S(2)}, u32[]{:S(2)}) %collective-permute-start.30) | collective-permute-done | bytes 524320 | tf_op jit(solution)/shard_map/ppermute | solution.py:10
  152.4 4.3 collective-permute-done.1
  164.9 14.3 %collective-permute-done.7 = bf16[16,128,128]{2,0,1:T(8,128)(2,1)S(1)} collective-permute-done((bf16[16,128,128]{2,0,1:T(8,128)(2,1)}, bf16[16,128,128]{2,0,1:T(8,128)(2,1)S(1)}, u32[]{:S(2)}, u32[]{:S(2)}) %collective-permute-start.7) | collective-permute-done | bytes 524320 | tf_op jit(solution)/shard_map/ppermute | solution.py:10
  183.6 3.6 collective-permute-start.16
  187.3 14.3 %collective-permute-done.11 = bf16[16,128,128]{2,0,1:T(8,128)(2,1)S(1)} collective-permute-done((bf16[16,128,128]{2,0,1:T(8,128)(2,1)}, bf16[16,128,128]{2,0,1:T(8,128)(2,1)S(1)}, u32[]{:S(2)}, u32[]{:S(2)}) %collective-permute-start.11) | collective-permute-done | bytes 524320 | tf_op jit(solution)/shard_map/ppermute | solution.py:10
  206.5 3.6 collective-permute-start.20
  210.2 13.9 %collective-permute-done.15 = bf16[16,128,128]{2,0,1:T(8,128)(2,1)S(1)} collective-permute-done((bf16[16,128,128]{2,0,1:T(8,128)(2,1)S(1)}, bf16[16,128,128]{2,0,1:T(8,128)(2,1)S(1)}, u32[]{:S(2)}, u32[]{:S(2)}) %collective-permute-start.15) | collective-permute-done | bytes 524320 | tf_op jit(solution)/shard_map/ppermute | solution.py:10
  232.3 14.3 %collective-permute-done.19 = bf16[16,128,128]{2,0,1:T(8,128)(2,1)S(1)} collective-permute-done((bf16[16,128,128]{2,0,1:T(8,128)(2,1)S(1)}, bf16[16,128,128]{2,0,1:T(8,128)(2,1)S(1)}, u32[]{:S(2)}, u32[]{:S(2)}) %collective-permute-start.19) | collective-permute-done | bytes 524320 | tf_op jit(solution)/shard_map/ppermute | solution.py:10
  254.7 14.3 %collective-permute-done.23 = bf16[16,128,128]{2,0,1:T(8,128)(2,1)S(1)} collective-permute-done((bf16[16,128,128]{2,0,1:T(8,128)(2,1)S(1)}, bf16[16,128,128]{2,0,1:T(8,128)(2,1)S(1)}, u32[]{:S(2)}, u32[]{:S(2)}) %collective-permute-start.23) | collective-permute-done | bytes 524320 | tf_op jit(solution)/shard_map/ppermute | solution.py:10
  277.4 14.2 %collective-permute-done.27 = bf16[16,128,128]{2,0,1:T(8,128)(2,1)S(1)} collective-permute-done((bf16[16,128,128]{2,0,1:T(8,128)(2,1)S(1)}, bf16[16,128,128]{2,0,1:T(8,128)(2,1)S(1)}, u32[]{:S(2)}, u32[]{:S(2)}) %collective-permute-start.27) | collective-permute-done | bytes 524320 | tf_op jit(solution)/shard_map/ppermute | solution.py:10
  299.3 14.7 %collective-permute-done.31 = bf16[16,128,128]{2,0,1:T(8,128)(2,1)S(1)} collective-permute-done((bf16[16,128,128]{2,0,1:T(8,128)(2,1)S(1)}, bf16[16,128,128]{2,0,1:T(8,128)(2,1)S(1)}, u32[]{:S(2)}, u32[]{:S(2)}) %collective-permute-start.31) | collective-permute-done | bytes 524320 | tf_op jit(solution)/shard_map/ppermute | solution.py:10
  326.0 3.6 collective-permute-start.35
  329.7 82.5 %collective-permute-done.34 = bf16[8,15,128,128]{3,2,1,0:T(8,128)(2,1)S(1)} collective-permute-done((bf16[8,15,128,128]{3,2,1,0:T(8,128)(2,1)S(1)}, bf16[8,15,128,128]{3,2,1,0:T(8,128)(2,1)S(1)}, u32[]{:S(2)}, u32[]{:S(2)}) %collective-permute-start.34) | collective-permute-done | bytes 3932192 | tf_op jit(solution)/shard_map/ppermute | solution.py:18
  414.7 4.7 %copy.52 = bf16[8,15,128,128]{3,1,2,0:T(8,128)(2,1)S(1)} copy(bf16[8,15,128,128]{3,2,1,0:T(8,128)(2,1)} %collective-permute-done.35) | data formatting | bytes 7864320 | tf_op jit(solution)/shard_map/ppermute | solution.py:21
  419.5 6.2 %pad_maximum_fusion = bf16[8,46,128,128]{3,1,2,0:T(8,128)(2,1)S(1)} fusion(bf16[8,15,128,128]{3,1,2,0:T(8,128)(2,1)S(1)} %copy.52, bf16[8,16,128,128]{3,1,2,0:T(8,128)(2,1)S(1)} %bitcast_dynamic-update-slice_fusion, bf16[8,15,128,128]{3,1,2,0:T(8,128)(2,1)S(1)} %copy.51), kind=kLoop, calls=%fused_computation | loop fusion | flops 36175872 | bytes 24117248 | tf_op jit(solution)/shard_map/concatenate | solution.py:22
  425.6 4.5 copy-done
  (224 shorter events, 161.9 us)
Async XLA Ops:
  2.6 46.2 %collective-permute-start.4 = (bf16[15,128,128]{2,1,0:T(8,128)(2,1)}, bf16[15,128,128]{2,1,0:T(8,128)(2,1)}, u32[]{:S(2)}, u32[]{:S(2)}) collective-permute-start(bf16[15,128,128]{2,1,0:T(8,128)(2,1)} %get-tuple-element.55), channel_id=1, source_target_pairs={{0,1},{1,2},{2,3},{3,4},{4,5},{5,6},{6,7},{7,8},{8,9},{9,10},{10,1... | collective-permute-start | bytes 1474568 | tf_op jit(solution)/shard_map/ppermute | solution.py:18
  4.5 46.4 %collective-permute-start.5 = (bf16[15,128,128]{2,1,0:T(8,128)(2,1)}, bf16[15,128,128]{2,1,0:T(8,128)(2,1)}, u32[]{:S(2)}, u32[]{:S(2)}) collective-permute-start(bf16[15,128,128]{2,1,0:T(8,128)(2,1)} %get-tuple-element.56), channel_id=1, source_target_pairs={{1,0},{2,1},{3,2},{4,3},{5,4},{6,5},{7,6},{8,7},{9,8},{10,9},{11,1... | collective-permute-start | bytes 1474568 | tf_op jit(solution)/shard_map/ppermute | solution.py:21
  12.0 69.5 %collective-permute-start = (bf16[16,128,128]{2,0,1:T(8,128)(2,1)}, bf16[16,128,128]{2,0,1:T(8,128)(2,1)}, u32[]{:S(2)}, u32[]{:S(2)}) collective-permute-start(bf16[16,128,128]{2,0,1:T(8,128)(2,1)} %bitcast.447), channel_id=1, source_target_pairs={{0,2},{1,3},{2,4},{3,5},{4,6},{5,7},{6,8},{7,9},{8,10},{9,11},{10,... | collective-permute-start | bytes 1572872 | tf_op jit(solution)/shard_map/ppermute | solution.py:10
  17.6 86.9 %collective-permute-start.6 = (bf16[16,128,128]{2,0,1:T(8,128)(2,1)}, bf16[16,128,128]{2,0,1:T(8,128)(2,1)}, u32[]{:S(2)}, u32[]{:S(2)}) collective-permute-start(bf16[16,128,128]{2,0,1:T(8,128)(2,1)} %bitcast.446), channel_id=1, source_target_pairs={{0,2},{1,3},{2,4},{3,5},{4,6},{5,7},{6,8},{7,9},{8,10},{9,11},{10,... | collective-permute-start | bytes 1572872 | tf_op jit(solution)/shard_map/ppermute | solution.py:10
  21.3 86.2 %collective-permute-start.10 = (bf16[16,128,128]{2,0,1:T(8,128)(2,1)}, bf16[16,128,128]{2,0,1:T(8,128)(2,1)}, u32[]{:S(2)}, u32[]{:S(2)}) collective-permute-start(bf16[16,128,128]{2,0,1:T(8,128)(2,1)} %bitcast.445), channel_id=1, source_target_pairs={{0,2},{1,3},{2,4},{3,5},{4,6},{5,7},{6,8},{7,9},{8,10},{9,11},{10,... | collective-permute-start | bytes 1572872 | tf_op jit(solution)/shard_map/ppermute | solution.py:10
  48.8 61.8 %collective-permute-start.14 = (bf16[16,128,128]{2,0,1:T(8,128)(2,1)}, bf16[16,128,128]{2,0,1:T(8,128)(2,1)}, u32[]{:S(2)}, u32[]{:S(2)}) collective-permute-start(bf16[16,128,128]{2,0,1:T(8,128)(2,1)} %bitcast.464), channel_id=1, source_target_pairs={{0,2},{1,3},{2,4},{3,5},{4,6},{5,7},{6,8},{7,9},{8,10},{9,11},{10,... | collective-permute-start | bytes 1572872 | tf_op jit(solution)/shard_map/ppermute | solution.py:10
  50.9 62.6 %collective-permute-start.18 = (bf16[16,128,128]{2,0,1:T(8,128)(2,1)}, bf16[16,128,128]{2,0,1:T(8,128)(2,1)}, u32[]{:S(2)}, u32[]{:S(2)}) collective-permute-start(bf16[16,128,128]{2,0,1:T(8,128)(2,1)} %bitcast.460), channel_id=1, source_target_pairs={{0,2},{1,3},{2,4},{3,5},{4,6},{5,7},{6,8},{7,9},{8,10},{9,11},{10,... | collective-permute-start | bytes 1572872 | tf_op jit(solution)/shard_map/ppermute | solution.py:10
  107.5 42.0 %collective-permute-start.30 = (bf16[16,128,128]{2,0,1:T(8,128)(2,1)}, bf16[16,128,128]{2,0,1:T(8,128)(2,1)S(1)}, u32[]{:S(2)}, u32[]{:S(2)}) collective-permute-start(bf16[16,128,128]{2,0,1:T(8,128)(2,1)} %bitcast.448), channel_id=1, source_target_pairs={{0,2},{1,3},{2,4},{3,5},{4,6},{5,7},{6,8},{7,9},{8,10},{9,11},{10,... | collective-permute-start | bytes 1572872 | tf_op jit(solution)/shard_map/ppermute | solution.py:10
  110.5 46.2 %collective-permute-start.1 = (bf16[16,128,128]{2,0,1:T(8,128)(2,1)}, bf16[16,128,128]{2,0,1:T(8,128)(2,1)S(1)}, u32[]{:S(2)}, u32[]{:S(2)}) collective-permute-start(bf16[16,128,128]{2,0,1:T(8,128)(2,1)} %bitcast.447), channel_id=1, source_target_pairs={{0,1},{1,2},{2,3},{3,4},{4,5},{5,6},{6,7},{7,8},{8,9},{9,10},{10,1... | collective-permute-start | bytes 1572872 | tf_op jit(solution)/shard_map/ppermute | solution.py:10
  113.6 45.5 %collective-permute-start.2 = (bf16[16,128,128]{2,0,1:T(8,128)(2,1)}, bf16[16,128,128]{2,0,1:T(8,128)(2,1)S(1)}, u32[]{:S(2)}, u32[]{:S(2)}) collective-permute-start(bf16[16,128,128]{2,0,1:T(8,128)(2,1)} %bitcast.447), channel_id=1, source_target_pairs={{1,0},{2,1},{3,2},{4,3},{5,4},{6,5},{7,6},{8,7},{9,8},{10,9},{11,1... | collective-permute-start | bytes 1572872 | tf_op jit(solution)/shard_map/ppermute | solution.py:10
  118.4 42.7 %collective-permute-start.3 = (bf16[16,128,128]{2,0,1:T(8,128)(2,1)}, bf16[16,128,128]{2,0,1:T(8,128)(2,1)S(1)}, u32[]{:S(2)}, u32[]{:S(2)}) collective-permute-start(bf16[16,128,128]{2,0,1:T(8,128)(2,1)} %bitcast.447), channel_id=1, source_target_pairs={{2,0},{3,1},{4,2},{5,3},{6,4},{7,5},{8,6},{9,7},{10,8},{11,9},{12,... | collective-permute-start | bytes 1572872 | tf_op jit(solution)/shard_map/ppermute | solution.py:10
  159.1 42.5 %collective-permute-start.11 = (bf16[16,128,128]{2,0,1:T(8,128)(2,1)}, bf16[16,128,128]{2,0,1:T(8,128)(2,1)S(1)}, u32[]{:S(2)}, u32[]{:S(2)}) collective-permute-start(bf16[16,128,128]{2,0,1:T(8,128)(2,1)} %bitcast.445), channel_id=1, source_target_pairs={{0,1},{1,2},{2,3},{3,4},{4,5},{5,6},{6,7},{7,8},{8,9},{9,10},{10,1... | collective-permute-start | bytes 1572872 | tf_op jit(solution)/shard_map/ppermute | solution.py:10
  161.1 42.9 %collective-permute-start.12 = (bf16[16,128,128]{2,0,1:T(8,128)(2,1)}, bf16[16,128,128]{2,0,1:T(8,128)(2,1)S(1)}, u32[]{:S(2)}, u32[]{:S(2)}) collective-permute-start(bf16[16,128,128]{2,0,1:T(8,128)(2,1)} %bitcast.445), channel_id=1, source_target_pairs={{1,0},{2,1},{3,2},{4,3},{5,4},{6,5},{7,6},{8,7},{9,8},{10,9},{11,1... | collective-permute-start | bytes 1572872 | tf_op jit(solution)/shard_map/ppermute | solution.py:10
  181.6 42.5 %collective-permute-start.15 = (bf16[16,128,128]{2,0,1:T(8,128)(2,1)S(1)}, bf16[16,128,128]{2,0,1:T(8,128)(2,1)S(1)}, u32[]{:S(2)}, u32[]{:S(2)}) collective-permute-start(bf16[16,128,128]{2,0,1:T(8,128)(2,1)S(1)} %bitcast.465), channel_id=1, source_target_pairs={{0,1},{1,2},{2,3},{3,4},{4,5},{5,6},{6,7},{7,8},{8,9},{9,10},{10,1... | collective-permute-start | bytes 1572872 | tf_op jit(solution)/shard_map/ppermute | solution.py:10
  183.6 42.9 %collective-permute-start.16 = (bf16[16,128,128]{2,0,1:T(8,128)(2,1)S(1)}, bf16[16,128,128]{2,0,1:T(8,128)(2,1)S(1)}, u32[]{:S(2)}, u32[]{:S(2)}) collective-permute-start(bf16[16,128,128]{2,0,1:T(8,128)(2,1)S(1)} %bitcast.466), channel_id=1, source_target_pairs={{1,0},{2,1},{3,2},{4,3},{5,4},{6,5},{7,6},{8,7},{9,8},{10,9},{11,1... | collective-permute-start | bytes 1572872 | tf_op jit(solution)/shard_map/ppermute | solution.py:10
  204.1 42.5 %collective-permute-start.19 = (bf16[16,128,128]{2,0,1:T(8,128)(2,1)S(1)}, bf16[16,128,128]{2,0,1:T(8,128)(2,1)S(1)}, u32[]{:S(2)}, u32[]{:S(2)}) collective-permute-start(bf16[16,128,128]{2,0,1:T(8,128)(2,1)S(1)} %bitcast.461), channel_id=1, source_target_pairs={{0,1},{1,2},{2,3},{3,4},{4,5},{5,6},{6,7},{7,8},{8,9},{9,10},{10,1... | collective-permute-start | bytes 1572872 | tf_op jit(solution)/shard_map/ppermute | solution.py:10
  206.5 42.5 %collective-permute-start.20 = (bf16[16,128,128]{2,0,1:T(8,128)(2,1)S(1)}, bf16[16,128,128]{2,0,1:T(8,128)(2,1)S(1)}, u32[]{:S(2)}, u32[]{:S(2)}) collective-permute-start(bf16[16,128,128]{2,0,1:T(8,128)(2,1)S(1)} %bitcast.462), channel_id=1, source_target_pairs={{1,0},{2,1},{3,2},{4,3},{5,4},{6,5},{7,6},{8,7},{9,8},{10,9},{11,1... | collective-permute-start | bytes 1572872 | tf_op jit(solution)/shard_map/ppermute | solution.py:10
  226.5 42.5 %collective-permute-start.23 = (bf16[16,128,128]{2,0,1:T(8,128)(2,1)S(1)}, bf16[16,128,128]{2,0,1:T(8,128)(2,1)S(1)}, u32[]{:S(2)}, u32[]{:S(2)}) collective-permute-start(bf16[16,128,128]{2,0,1:T(8,128)(2,1)S(1)} %bitcast.457), channel_id=1, source_target_pairs={{0,1},{1,2},{2,3},{3,4},{4,5},{5,6},{6,7},{7,8},{8,9},{9,10},{10,1... | collective-permute-start | bytes 1572872 | tf_op jit(solution)/shard_map/ppermute | solution.py:10
  228.6 42.8 %collective-permute-start.24 = (bf16[16,128,128]{2,0,1:T(8,128)(2,1)S(1)}, bf16[16,128,128]{2,0,1:T(8,128)(2,1)S(1)}, u32[]{:S(2)}, u32[]{:S(2)}) collective-permute-start(bf16[16,128,128]{2,0,1:T(8,128)(2,1)S(1)} %bitcast.458), channel_id=1, source_target_pairs={{1,0},{2,1},{3,2},{4,3},{5,4},{6,5},{7,6},{8,7},{9,8},{10,9},{11,1... | collective-permute-start | bytes 1572872 | tf_op jit(solution)/shard_map/ppermute | solution.py:10
  249.0 42.5 %collective-permute-start.27 = (bf16[16,128,128]{2,0,1:T(8,128)(2,1)S(1)}, bf16[16,128,128]{2,0,1:T(8,128)(2,1)S(1)}, u32[]{:S(2)}, u32[]{:S(2)}) collective-permute-start(bf16[16,128,128]{2,0,1:T(8,128)(2,1)S(1)} %bitcast.453), channel_id=1, source_target_pairs={{0,1},{1,2},{2,3},{3,4},{4,5},{5,6},{6,7},{7,8},{8,9},{9,10},{10,1... | collective-permute-start | bytes 1572872 | tf_op jit(solution)/shard_map/ppermute | solution.py:10
  251.0 42.9 %collective-permute-start.28 = (bf16[16,128,128]{2,0,1:T(8,128)(2,1)S(1)}, bf16[16,128,128]{2,0,1:T(8,128)(2,1)S(1)}, u32[]{:S(2)}, u32[]{:S(2)}) collective-permute-start(bf16[16,128,128]{2,0,1:T(8,128)(2,1)S(1)} %bitcast.454), channel_id=1, source_target_pairs={{1,0},{2,1},{3,2},{4,3},{5,4},{6,5},{7,6},{8,7},{9,8},{10,9},{11,1... | collective-permute-start | bytes 1572872 | tf_op jit(solution)/shard_map/ppermute | solution.py:10
  271.5 42.5 %collective-permute-start.31 = (bf16[16,128,128]{2,0,1:T(8,128)(2,1)S(1)}, bf16[16,128,128]{2,0,1:T(8,128)(2,1)S(1)}, u32[]{:S(2)}, u32[]{:S(2)}) collective-permute-start(bf16[16,128,128]{2,0,1:T(8,128)(2,1)S(1)} %bitcast.449), channel_id=1, source_target_pairs={{0,1},{1,2},{2,3},{3,4},{4,5},{5,6},{6,7},{7,8},{8,9},{9,10},{10,1... | collective-permute-start | bytes 1572872 | tf_op jit(solution)/shard_map/ppermute | solution.py:10
  323.0 89.1 %collective-permute-start.34 = (bf16[8,15,128,128]{3,2,1,0:T(8,128)(2,1)S(1)}, bf16[8,15,128,128]{3,2,1,0:T(8,128)(2,1)S(1)}, u32[]{:S(2)}, u32[]{:S(2)}) collective-permute-start(bf16[8,15,128,128]{3,2,1,0:T(8,128)(2,1)S(1)} %copy.49), channel_id=1, source_target_pairs={{0,1},{1,2},{2,3},{3,4},{4,5},{5,6},{6,7},{7,8},{8,9},{9,10},{10,1... | collective-permute-start | bytes 11796488 | tf_op jit(solution)/shard_map/ppermute | solution.py:18
  326.0 88.7 %collective-permute-start.35 = (bf16[8,15,128,128]{3,2,1,0:T(8,128)(2,1)S(1)}, bf16[8,15,128,128]{3,2,1,0:T(8,128)(2,1)}, u32[]{:S(2)}, u32[]{:S(2)}) collective-permute-start(bf16[8,15,128,128]{3,2,1,0:T(8,128)(2,1)S(1)} %copy.50), channel_id=1, source_target_pairs={{1,0},{2,1},{3,2},{4,3},{5,4},{6,5},{7,6},{8,7},{9,8},{10,9},{11,1... | collective-permute-start | bytes 11796488 | tf_op jit(solution)/shard_map/ppermute | solution.py:21
  (51 other events, 762.4 us)
where the time goes:
time: 465 us; the launch traced here: 458 us
  waiting for transfers between devices  208 us (45%)
  starting transfers between devices  115 us (25%)
  matrix products  64.5 us (14%)
  local copies, waits for them, and re-layouts  41.7 us (9%)
  other arithmetic  16.8 us (4%)
  between operations  11.4 us (2%)
    ppermute x32, waiting for transfers between devices, passed_along(): lax.ppermute(value, axis, [(source, source + steps) for source in range(i...  126 us
    ppermute x32, starting transfers between devices, passed_along(): lax.ppermute(value, axis, [(source, source + steps) for source in range(i...  104 us
    ppermute x2, waiting for transfers between devices, extended(): lax.ppermute(lax.slice_in_dim(block, block.shape[dim] - width, None, axis...  82.5 us
    dot_general x8, matrix products, forward(): jnp.einsum('wyz,yk->wkz', blur_z, y_matrix, preferred_element_type=jnp.fl...  28.5 us
    unnamed x118, local copies, waits for them, and re-layouts  24.9 us
    dot_general x8, matrix products, adjoint(): jnp.einsum('wyz,wi->iyz', window, x_matrix, preferred_element_type=jnp.fl...  16.7 us
    dot_general x8, matrix products, adjoint(): jnp.einsum('xyk,zk->xyz', back_y, z_matrix, preferred_element_type=jnp.fl...  10.5 us
  transfers between devices with their start and end apart: 36, of which 14 were waited for; matrix products, arithmetic and copies ran while one was open for 16% of the time, Pallas kernels for 0%

commit v1 on v0

v1 whole, which is shorter than its diff:
```python
import functools

import jax
import jax.numpy as jnp
from jax import lax
from jax.experimental import pallas as pl
from jax.experimental.pallas import tpu as pltpu
from jax.sharding import PartitionSpec as P

SHIFT = 32
F32 = jnp.float32
BF16 = jnp.bfloat16
HALF = jnp.float16
MESH = pl.DeviceIdType.MESH


def moved(value, axis, steps):
    count = lax.axis_size(axis)
    pairs = [(source, source + steps) for source in range(count) if 0 <= source + steps < count]
    return lax.ppermute(value, axis, pairs)


def greet(count, me, hops):
    barrier = pltpu.get_barrier_semaphore()
    for k in range(1, hops + 1):
        for step in (k, -k):
            there = me + step

            @pl.when((there >= 0) & (there < count))
            def _():
                pl.semaphore_signal(
                    barrier, inc=1, device_id={"blocks": there}, device_id_type=MESH
                )

    pl.semaphore_wait(barrier, jnp.minimum(me, hops) + jnp.minimum(count - 1 - me, hops))


def window_kernel(count, hops, own_ref, out_ref, send_sem, recv_sem):
    me = lax.axis_index("blocks")
    greet(count, me, hops)
    order = [s for k in range(hops, 0, -1) for s in (k, -k)]

    def copy(step):
        return pltpu.make_async_remote_copy(
            src_ref=own_ref,
            dst_ref=out_ref.at[hops - step],
            send_sem=send_sem.at[hops - step],
            recv_sem=recv_sem.at[hops - step],
            device_id={"blocks": me + step},
            device_id_type=MESH,
        )

    for step in order:
        there = me + step

        @pl.when((there >= 0) & (there < count))
        def _():
            copy(step).start()

    out_ref[hops] = own_ref[...]
    for step in order:
        here = me - step

        @pl.when((here < 0) | (here >= count))
        def _():
            out_ref[hops - step] = jnp.zeros(own_ref.shape, own_ref.dtype)

    for step in order:
        there = me + step
        here = me - step

        @pl.when((there >= 0) & (there < count))
        def _():
            copy(step).wait_send()

        @pl.when((here >= 0) & (here < count))
        def _():
            copy(step).wait_recv()


def view_kernel(
    dims, win_ref, img_ref, xm_ref, xt_ref, tap_ref, extra_ref, own_ref, part_ref, held, low, mats
):
    views, rows, across, along, hops, margin = dims
    group = 16
    r = lax.broadcasted_iota(jnp.int32, (along, along), 0)
    c = lax.broadcasted_iota(jnp.int32, (along, along), 1)
    near = jnp.abs(r - c) <= margin

    @pl.loop(0, views)
    def _(v):
        for kind in range(4):
            line = jnp.broadcast_to(tap_ref[v, pl.ds(kind, 1), :], (along, along))
            turned = pltpu.roll(line, 0, 1, stride=1, stride_axis=0)
            mats[v, kind] = jnp.where(near, turned, 0.0).astype(BF16)

    @pl.loop(0, across // group)
    def _(g):
        base = pl.multiple_of(g * group, group)
        slabs = []
        for p in range(group):
            piece = win_ref[:, base + p].reshape(win_ref.shape[0] * rows, along)
            slabs.append(jnp.dot(xm_ref[...], piece, preferred_element_type=F32).astype(BF16))
        held[:, pl.ds(base, group), :] = jnp.swapaxes(jnp.stack(slabs), 0, 1)

    some = 4
    per = rows // some

    def both(left, block):
        outs = []
        for i in range(0, some, 2):
            pair = jnp.concatenate([block[i], block[i + 1]], axis=1)
            res = jnp.dot(left, pair, preferred_element_type=F32)
            outs += [res[:, :along], res[:, along:]]
        return outs

    @pl.loop(0, views * per)
    def _(t):
        v = t // per
        first = pl.multiple_of(t * some, some)
        inside = (t % per) * some
        block = held[pl.ds(first, some)].reshape(some * across, along)
        blur_z = jnp.dot(block, mats[v, 0], preferred_element_type=F32).astype(BF16)
        predicted = both(mats[v, 2], blur_z.reshape(some, across, along))
        ratios = []
        for i in range(some):
            image = img_ref[v, inside + i].astype(F32)
            ratios.append((image / (predicted[i] + extra_ref[first + i])).astype(BF16))
        ratio = jnp.concatenate(ratios, axis=0)
        back_z = jnp.dot(ratio, mats[v, 1], preferred_element_type=F32).astype(BF16)
        back = both(mats[v, 3], back_z.reshape(some, across, along))
        for i in range(some):
            top = back[i].astype(BF16)
            held[first + i] = top
            low[first + i] = (back[i] - top.astype(F32)).astype(BF16)

    @pl.loop(0, across // group)
    def _(g):
        base = pl.multiple_of(g * group, group)
        tops = jnp.swapaxes(held[:, pl.ds(base, group), :], 0, 1)
        lows = jnp.swapaxes(low[:, pl.ds(base, group), :], 0, 1)
        for p in range(group):
            stacked = jnp.concatenate([tops[p], lows[p]], axis=0)
            res = jnp.dot(xt_ref[...], stacked, preferred_element_type=F32)
            res = res.reshape(2 * hops + 1, rows, along)
            own_ref[base + p] = res[hops]
            for k in range(hops):
                part_ref[k, base + p] = res[k].astype(part_ref.dtype)
                part_ref[hops + k, base + p] = res[hops + 1 + k].astype(part_ref.dtype)


def vmem(n):
    return [pl.BlockSpec(memory_space=pltpu.VMEM)] * n


def taken(taps, index):
    match = index[..., None] == jnp.arange(taps.shape[-1])
    return jnp.sum(jnp.where(match, taps.astype(F32), 0.0), axis=-1)


def body(estimate, images, point_spread, shifts):
    views = images.shape[0]
    rows, across, along = estimate.shape
    taps = point_spread.shape[2]
    margin = taps // 2
    count = lax.axis_size("blocks")
    hops = -(-(margin + SHIFT) // rows)
    width = rows * (2 * hops + 1)
    slab = rows * count
    kernel = (point_spread / jnp.sum(point_spread, axis=2, keepdims=True)).astype(BF16)

    place = (jnp.arange(along) + along // 2) % along - along // 2
    plus = margin + place
    minus = margin - place
    lines = jnp.stack([minus, plus, plus, minus])
    which = jnp.stack([kernel[:, 2], kernel[:, 2], kernel[:, 1], kernel[:, 1]], axis=1)
    tap_lines = taken(which[:, :, None, :], lines[None])

    own = lax.axis_index("blocks") * rows + jnp.arange(rows)[None, :] - shifts[:, None]
    valid = (own >= 0) & (own < slab)
    index = (
        jnp.arange(width)[None, None, :]
        - jnp.arange(rows)[None, :, None]
        + shifts[:, None, None]
        + (margin - rows * hops)
    )
    x_mat = jnp.where(valid[:, :, None], taken(kernel[:, 0][:, None, None, :], index), 0.0)
    x_mat = x_mat.astype(BF16).reshape(views * rows, width)
    x_turned = x_mat.T
    x_twice = jnp.concatenate([x_turned, x_turned], axis=1)
    extra = jnp.where(valid, 0.0, 1.0).astype(F32).reshape(views * rows)

    block = (across, rows, along)
    mine = jnp.swapaxes(estimate.astype(BF16), 0, 1)
    window = pl.pallas_call(
        functools.partial(window_kernel, count, hops),
        out_shape=jax.ShapeDtypeStruct((2 * hops + 1,) + block, BF16),
        in_specs=vmem(1),
        out_specs=vmem(1)[0],
        scratch_shapes=[
            pltpu.SemaphoreType.DMA((2 * hops + 1,)),
            pltpu.SemaphoreType.DMA((2 * hops + 1,)),
        ],
        compiler_params=pltpu.CompilerParams(collective_id=0, has_side_effects=True),
        name="window",
    )(mine)

    dims = (views, rows, across, along, hops, margin)
    own_sum, parts = pl.pallas_call(
        functools.partial(view_kernel, dims),
        out_shape=(
            jax.ShapeDtypeStruct(block, F32),
            jax.ShapeDtypeStruct((2 * hops,) + block, F32),
        ),
        in_specs=vmem(5) + [pl.BlockSpec(memory_space=pltpu.SMEM)],
        out_specs=tuple(vmem(2)),
        scratch_shapes=[
            pltpu.VMEM((views * rows, across, along), BF16),
            pltpu.VMEM((views * rows, across, along), BF16),
            pltpu.VMEM((views, 4, along, along), BF16),
        ],
        compiler_params=pltpu.CompilerParams(vmem_limit_bytes=56 * 1024 * 1024),
        name="views",
    )(window, images, x_mat, x_twice, tap_lines, extra)

    sent = parts.astype(HALF)
    summed = own_sum
    for k in range(hops):
        summed = summed + moved(sent[hops + k], "blocks", k + 1).astype(F32)
        summed = summed + moved(sent[hops - 1 - k], "blocks", -k - 1).astype(F32)
    return estimate * jnp.swapaxes(summed, 0, 1) / views


def solution(mesh):
    in_specs = (
        P(("groups", "blocks"), None, None),
        P(None, ("groups", "blocks"), None, None),
        P(),
        P(),
    )
    out_specs = P(("groups", "blocks"), None, None)
    return jax.shard_map(body, mesh=mesh, in_specs=in_specs, out_specs=out_specs, check_vma=False)
```

time: 465 us -> 154 us (0.33)
  the two profiles are of different devices: /device:TPU:22 before, /device:TPU:0 now
where the time goes in v1:
time: 154 us
  Pallas kernels  88.6 us (58%)
  waiting for transfers between devices  33.6 us (22%)
  starting transfers between devices  16.2 us (11%)
  other arithmetic  8.26 us (5%)
  local copies, waits for them, and re-layouts  7.04 us (5%)
    pallas_call x1, Pallas kernels, body(): pl.pallas_call(functools.partial(window_kernel, count, hops), out_shape=j...  51.5 us
    pallas_call x1, Pallas kernels, body(): pl.pallas_call(functools.partial(view_kernel, dims), out_shape=(jax.Shape...  37.1 us
    ppermute x6, waiting for transfers between devices, moved(): return lax.ppermute(value, axis, pairs)  33.6 us
    ppermute x6, starting transfers between devices, moved(): return lax.ppermute(value, axis, pairs)  16.2 us
    convert_element_type x1, other arithmetic, body(): sent = parts.astype(HALF)  3.2 us
  transfers between devices with their start and end apart: 6, of which 2 were waited for; matrix products, arithmetic and copies ran while one was open for 0% of the time, Pallas kernels for 0%

profile of v1, /device:TPU:0, one launch (start us, length us, event | category | flops | bytes accessed | tf_op | source)
XLA Modules:
  0.0 153.9 jit_solution(2719931640701454736)
XLA Ops:
  0.0 0.8 reduce_sum.29
  0.8 0.8 divide_convert_fusion
  1.6 0.7 sub.65
  2.5 0.7 add_add_fusion
  3.2 0.3 select_reduce_fusion
  3.8 0.5 and_select_fusion.extra_ref
  4.7 0.6 copy.20.tap_ref
  5.3 0.7 copy.19.xm_ref
  6.0 0.6 pad_maximum_fusion.xt_ref
  6.7 2.6 %copy.27 = bf16[16,128,128]{2,0,1:T(8,128)(2,1)} copy(f32[16,128,128]{2,1,0:T(8,128)} %param.4) | data formatting | bytes 1572864 | tf_op args[0]
  9.3 51.5 %window.1.win_ref = bf16[7,128,16,128]{3,2,1,0:T(8,128)(2,1)} custom-call(bf16[128,16,128]{2,1,0:T(8,128)(2,1)} %bitcast.29), custom_call_target="tpu_custom_call" | custom-call | tf_op jit(solution)/shard_map/window/pallas_call | solution.py:195
  60.8 37.1 %views.1 = (f32[128,16,128]{2,1,0:T(8,128)}, f32[6,128,16,128]{3,2,1,0:T(8,128)}) custom-call(bf16[7,128,16,128]{3,2,1,0:T(8,128)(2,1)} %window.1.win_ref, bf16[8,16,128,128]{3,2,1,0:T(8,128)(2,1)} %img_ref.1, bf16[128,112]{1,0:T(8,128)(2,1)} %copy.19.xm_ref, bf16[112,256]{1,0:T(8,128)(2,1)} %pad_maximum_fusion.xt_ref, f32[8,4,128]{2,1,0:T(4,128)} %copy.20.tap_ref, ...), custom_call_target="tpu_custom_call" | custom-call | tf_op jit(solution)/shard_map/views/pallas_call | solution.py:209
  97.9 3.2 %convert_element_type.56 = f16[6,128,16,128]{3,2,1,0:T(8,128)(2,1)S(1)} convert(f32[6,128,16,128]{3,2,1,0:T(8,128)} %get-tuple-element.8) | non-fusion elementwise | flops 1572864 | bytes 9437184 | tf_op jit(solution)/shard_map/convert_element_type | solution.py:226
  101.1 0.6 slice_bitcast_fusion.5
  101.8 1.6 %collective-permute-start = (f16[128,16,128]{2,1,0:T(8,128)(2,1)S(1)}, f16[128,16,128]{2,1,0:T(8,128)(2,1)S(1)}, u32[]{:S(2)}, u32[]{:S(2)}) collective-permute-start(f16[128,16,128]{2,1,0:T(8,128)(2,1)S(1)} %get-tuple-element.9), channel_id=1, source_target_pairs={{0,1},{1,2},{2,3},{3,4},{4,5},{5,6},{6,7},{7,8},{8,9},{9,10},{10,1... | collective-permute-start | bytes 1572872 | tf_op jit(solution)/shard_map/ppermute | solution.py:20
  103.3 1.3 collective-permute-start.5
  104.6 5.7 %collective-permute-start.4 = (f16[128,16,128]{2,1,0:T(8,128)(2,1)S(1)}, f16[128,16,128]{2,1,0:T(8,128)(2,1)S(1)}, u32[]{:S(2)}, u32[]{:S(2)}) collective-permute-start(f16[128,16,128]{2,1,0:T(8,128)(2,1)S(1)} %get-tuple-element.11), channel_id=1, source_target_pairs={{0,3},{1,4},{2,5},{3,6},{4,7},{5,8},{6,9},{7,10},{8,11},{9,12},{10... | collective-permute-start | bytes 1572872 | tf_op jit(solution)/shard_map/ppermute | solution.py:20
  110.3 1.3 collective-permute-start.3
  111.6 5.0 %collective-permute-start.2 = (f16[128,16,128]{2,1,0:T(8,128)(2,1)S(1)}, f16[128,16,128]{2,1,0:T(8,128)(2,1)S(1)}, u32[]{:S(2)}, u32[]{:S(2)}) collective-permute-start(f16[128,16,128]{2,1,0:T(8,128)(2,1)S(1)} %get-tuple-element.13), channel_id=1, source_target_pairs={{0,2},{1,3},{2,4},{3,5},{4,6},{5,7},{6,8},{7,9},{8,10},{9,11},{10,... | collective-permute-start | bytes 1572872 | tf_op jit(solution)/shard_map/ppermute | solution.py:20
  116.7 1.3 collective-permute-start.1
  118.0 25.9 %collective-permute-done.4 = f16[128,16,128]{2,1,0:T(8,128)(2,1)S(1)} collective-permute-done((f16[128,16,128]{2,1,0:T(8,128)(2,1)S(1)}, f16[128,16,128]{2,1,0:T(8,128)(2,1)S(1)}, u32[]{:S(2)}, u32[]{:S(2)}) %collective-permute-start.4) | collective-permute-done | bytes 524320 | tf_op jit(solution)/shard_map/ppermute | solution.py:20
  143.9 7.7 %collective-permute-done.2 = f16[128,16,128]{2,1,0:T(8,128)(2,1)S(1)} collective-permute-done((f16[128,16,128]{2,1,0:T(8,128)(2,1)S(1)}, f16[128,16,128]{2,1,0:T(8,128)(2,1)S(1)}, u32[]{:S(2)}, u32[]{:S(2)}) %collective-permute-start.2) | collective-permute-done | bytes 524320 | tf_op jit(solution)/shard_map/ppermute | solution.py:20
  151.6 1.0 fusion
  152.6 1.3 copy.22
  (26 shorter events, 0.8 us)
Async XLA Ops:
  101.1 50.5 %copy-start = (f32[16,128,128]{2,1,0:T(8,128)S(1)}, f32[16,128,128]{2,1,0:T(8,128)}, u32[]{:S(2)}) copy-start(f32[16,128,128]{2,1,0:T(8,128)} %param.4) | copy-start | bytes 3145732
  101.1 50.5 %copy-start.1 = (f32[128,16,128]{2,1,0:T(8,128)S(1)}, f32[128,16,128]{2,1,0:T(8,128)}, u32[]{:S(2)}) copy-start(f32[128,16,128]{2,1,0:T(8,128)} %get-tuple-element.7) | copy-start | bytes 3145732
  101.8 14.9 %collective-permute-start = (f16[128,16,128]{2,1,0:T(8,128)(2,1)S(1)}, f16[128,16,128]{2,1,0:T(8,128)(2,1)S(1)}, u32[]{:S(2)}, u32[]{:S(2)}) collective-permute-start(f16[128,16,128]{2,1,0:T(8,128)(2,1)S(1)} %get-tuple-element.9), channel_id=1, source_target_pairs={{0,1},{1,2},{2,3},{3,4},{4,5},{5,6},{6,7},{7,8},{8,9},{9,10},{10,1... | collective-permute-start | bytes 1572872 | tf_op jit(solution)/shard_map/ppermute | solution.py:20
  103.3 14.7 %collective-permute-start.5 = (f16[128,16,128]{2,1,0:T(8,128)(2,1)S(1)}, f16[128,16,128]{2,1,0:T(8,128)(2,1)S(1)}, u32[]{:S(2)}, u32[]{:S(2)}) collective-permute-start(f16[128,16,128]{2,1,0:T(8,128)(2,1)S(1)} %get-tuple-element.10), channel_id=1, source_target_pairs={{3,0},{4,1},{5,2},{6,3},{7,4},{8,5},{9,6},{10,7},{11,8},{12,9},{13... | collective-permute-start | bytes 1572872 | tf_op jit(solution)/shard_map/ppermute | solution.py:20
  104.6 39.3 %collective-permute-start.4 = (f16[128,16,128]{2,1,0:T(8,128)(2,1)S(1)}, f16[128,16,128]{2,1,0:T(8,128)(2,1)S(1)}, u32[]{:S(2)}, u32[]{:S(2)}) collective-permute-start(f16[128,16,128]{2,1,0:T(8,128)(2,1)S(1)} %get-tuple-element.11), channel_id=1, source_target_pairs={{0,3},{1,4},{2,5},{3,6},{4,7},{5,8},{6,9},{7,10},{8,11},{9,12},{10... | collective-permute-start | bytes 1572872 | tf_op jit(solution)/shard_map/ppermute | solution.py:20
  110.3 33.6 %collective-permute-start.3 = (f16[128,16,128]{2,1,0:T(8,128)(2,1)S(1)}, f16[128,16,128]{2,1,0:T(8,128)(2,1)S(1)}, u32[]{:S(2)}, u32[]{:S(2)}) collective-permute-start(f16[128,16,128]{2,1,0:T(8,128)(2,1)S(1)} %get-tuple-element.12), channel_id=1, source_target_pairs={{2,0},{3,1},{4,2},{5,3},{6,4},{7,5},{8,6},{9,7},{10,8},{11,9},{12,... | collective-permute-start | bytes 1572872 | tf_op jit(solution)/shard_map/ppermute | solution.py:20
  111.6 40.0 %collective-permute-start.2 = (f16[128,16,128]{2,1,0:T(8,128)(2,1)S(1)}, f16[128,16,128]{2,1,0:T(8,128)(2,1)S(1)}, u32[]{:S(2)}, u32[]{:S(2)}) collective-permute-start(f16[128,16,128]{2,1,0:T(8,128)(2,1)S(1)} %get-tuple-element.13), channel_id=1, source_target_pairs={{0,2},{1,3},{2,4},{3,5},{4,6},{5,7},{6,8},{7,9},{8,10},{9,11},{10,... | collective-permute-start | bytes 1572872 | tf_op jit(solution)/shard_map/ppermute | solution.py:20
  116.7 34.9 %collective-permute-start.1 = (f16[128,16,128]{2,1,0:T(8,128)(2,1)S(1)}, f16[128,16,128]{2,1,0:T(8,128)(2,1)S(1)}, u32[]{:S(2)}, u32[]{:S(2)}) collective-permute-start(f16[128,16,128]{2,1,0:T(8,128)(2,1)S(1)} %get-tuple-element.14), channel_id=1, source_target_pairs={{1,0},{2,1},{3,2},{4,3},{5,4},{6,5},{7,6},{8,7},{9,8},{10,9},{11,1... | collective-permute-start | bytes 1572872 | tf_op jit(solution)/shard_map/ppermute | solution.py:20

commit v2 on v1

--- a/solution.py
+++ b/solution.py
@@ -14,72 +14,94 @@
 MESH = pl.DeviceIdType.MESH
 
 
-def moved(value, axis, steps):
-    count = lax.axis_size(axis)
-    pairs = [(source, source + steps) for source in range(count) if 0 <= source + steps < count]
-    return lax.ppermute(value, axis, pairs)
-
-
-def greet(count, me, hops):
-    barrier = pltpu.get_barrier_semaphore()
-    for k in range(1, hops + 1):
-        for step in (k, -k):
-            there = me + step
-
-            @pl.when((there >= 0) & (there < count))
-            def _():
-                pl.semaphore_signal(
-                    barrier, inc=1, device_id={"blocks": there}, device_id_type=MESH
-                )
-
-    pl.semaphore_wait(barrier, jnp.minimum(me, hops) + jnp.minimum(count - 1 - me, hops))
-
-
-def window_kernel(count, hops, own_ref, out_ref, send_sem, recv_sem):
+def window_kernel(count, own_ref, out_ref, send_sem, recv_sem):
     me = lax.axis_index("blocks")
-    greet(count, me, hops)
-    order = [s for k in range(hops, 0, -1) for s in (k, -k)]
-
-    def copy(step):
+    odd = lax.rem(me, 2)
+    mid = 3
+
+    def send(src, slot, there, sem):
         return pltpu.make_async_remote_copy(
-            src_ref=own_ref,
-            dst_ref=out_ref.at[hops - step],
-            send_sem=send_sem.at[hops - step],
-            recv_sem=recv_sem.at[hops - step],
-            device_id={"blocks": me + step},
+            src_ref=src,
+            dst_ref=out_ref.at[slot],
+            send_sem=send_sem.at[sem],
+            recv_sem=recv_sem.at[slot],
+            device_id={"blocks": there},
             device_id_type=MESH,
         )
 
-    for step in order:
-        there = me + step
-
-        @pl.when((there >= 0) & (there < count))
-        def _():
-            copy(step).start()
-
-    out_ref[hops] = own_ref[...]
-    for step in order:
-        here = me - step
-
-        @pl.when((here < 0) | (here >= count))
-        def _():
-            out_ref[hops - step] = jnp.zeros(own_ref.shape, own_ref.dtype)
-
-    for step in order:
-        there = me + step
-        here = me - step
-
-        @pl.when((there >= 0) & (there < count))
-        def _():
-            copy(step).wait_send()
-
-        @pl.when((here >= 0) & (here < count))
-        def _():
-            copy(step).wait_recv()
+    def run(mate, far):
+        low = me >= 2
+        high = me + 2 < count
+        away = (me + far >= 0) & (me + far < count)
+        barrier = pltpu.get_barrier_semaphore()
+
+        def signal(there):
+            pl.semaphore_signal(barrier, inc=1, device_id={"blocks": there}, device_id_type=MESH)
+
+        signal(me + mate)
+        pl.when(low)(lambda: signal(me - 2))
+        pl.when(high)(lambda: signal(me + 2))
+        pl.when(away)(lambda: signal(me + far))
+        peers = 1 + low.astype(jnp.int32) + high.astype(jnp.int32) + away.astype(jnp.int32)
+        pl.semaphore_wait(barrier, peers)
+
+        down = send(own_ref, mid + 2, me - 2, 0)
+        up = send(own_ref, mid - 2, me + 2, 1)
+        long = send(own_ref, mid - far, me + far, 2)
+        near = send(own_ref, mid - mate, me + mate, 3)
+        pass_low = send(out_ref.at[mid - 2], mid - 2 - mate, me + mate, 4)
+        pass_high = send(out_ref.at[mid + 2], mid + 2 - mate, me + mate, 5)
+        pl.when(low)(down.start)
+        pl.when(high)(up.start)
+        pl.when(away)(long.start)
+        near.start()
+
+        out_ref[mid] = own_ref[...]
+        for offset in (-3, -2, -1, 1, 2, 3):
+            if offset != mate:
+                there = me + offset
+
+                @pl.when((there < 0) | (there >= count))
+                def _():
+                    out_ref[mid + offset] = jnp.zeros(own_ref.shape, own_ref.dtype)
+
+        @pl.when(low)
+        def _():
+            up.wait_recv()
+            pass_low.start()
+
+        @pl.when(high)
+        def _():
+            down.wait_recv()
+            pass_high.start()
+
+        send(own_ref, mid + mate, me + mate, 3).wait_recv()
+
+        @pl.when(low)
+        def _():
+            send(own_ref, mid - 2 + mate, me + mate, 4).wait_recv()
+            pass_low.wait_send()
+            down.wait_send()
+
+        @pl.when(high)
+        def _():
+            send(own_ref, mid + 2 + mate, me + mate, 5).wait_recv()
+            pass_high.wait_send()
+            up.wait_send()
+
+        @pl.when(away)
+        def _():
+            send(own_ref, mid + far, me + far, 2).wait_recv()
+            long.wait_send()
+
+        near.wait_send()
+
+    pl.when(odd == 0)(lambda: run(1, -3))
+    pl.when(odd == 1)(lambda: run(-1, 3))
 
 
 def view_kernel(
-    dims, win_ref, img_ref, xm_ref, xt_ref, tap_ref, extra_ref, own_ref, part_ref, held, low, mats
+    dims, win_ref, img_ref, xm_ref, xt_ref, tap_ref, extra_ref, odd_ref, keep_ref, mate_ref, far_ref, held, low, mats
 ):
     views, rows, across, along, hops, margin = dims
     group = 16
@@ -143,10 +165,20 @@
             stacked = jnp.concatenate([tops[p], lows[p]], axis=0)
             res = jnp.dot(xt_ref[...], stacked, preferred_element_type=F32)
             res = res.reshape(2 * hops + 1, rows, along)
-            own_ref[base + p] = res[hops]
-            for k in range(hops):
-                part_ref[k, base + p] = res[k].astype(part_ref.dtype)
-                part_ref[hops + k, base + p] = res[hops + 1 + k].astype(part_ref.dtype)
+            for k in range(3):
+                keep_ref[k, base + p] = res[2 * k + 1]
+
+            @pl.when(odd_ref[0] == 0)
+            def _():
+                for k in range(3):
+                    mate_ref[k, base + p] = res[2 * k + 2]
+                far_ref[base + p] = res[0]
+
+            @pl.when(odd_ref[0] == 1)
+            def _():
+                for k in range(3):
+                    mate_ref[k, base + p] = res[2 * k]
+                far_ref[base + p] = res[6]
 
 
 def vmem(n):
@@ -190,10 +222,12 @@
     x_twice = jnp.concatenate([x_turned, x_turned], axis=1)
     extra = jnp.where(valid, 0.0, 1.0).astype(F32).reshape(views * rows)
 
+    odd = lax.rem(lax.axis_index("blocks"), 2).astype(jnp.int32).reshape(1)
+
     block = (across, rows, along)
     mine = jnp.swapaxes(estimate.astype(BF16), 0, 1)
     window = pl.pallas_call(
-        functools.partial(window_kernel, count, hops),
+        functools.partial(window_kernel, count),
         out_shape=jax.ShapeDtypeStruct((2 * hops + 1,) + block, BF16),
         in_specs=vmem(1),
         out_specs=vmem(1)[0],
@@ -206,14 +240,15 @@
     )(mine)
 
     dims = (views, rows, across, along, hops, margin)
-    own_sum, parts = pl.pallas_call(
+    keep, mates, far = pl.pallas_call(
         functools.partial(view_kernel, dims),
         out_shape=(
+            jax.ShapeDtypeStruct((3,) + block, F32),
+            jax.ShapeDtypeStruct((3,) + block, F32),
             jax.ShapeDtypeStruct(block, F32),
-            jax.ShapeDtypeStruct((2 * hops,) + block, F32),
         ),
-        in_specs=vmem(5) + [pl.BlockSpec(memory_space=pltpu.SMEM)],
-        out_specs=tuple(vmem(2)),
+        in_specs=vmem(5) + [pl.BlockSpec(memory_space=pltpu.SMEM)] * 2,
+        out_specs=tuple(vmem(3)),
         scratch_shapes=[
             pltpu.VMEM((views * rows, across, along), BF16),
             pltpu.VMEM((views * rows, across, along), BF16),
@@ -221,13 +256,16 @@
         ],
         compiler_params=pltpu.CompilerParams(vmem_limit_bytes=56 * 1024 * 1024),
         name="views",
-    )(window, images, x_mat, x_twice, tap_lines, extra)
-
-    sent = parts.astype(HALF)
-    summed = own_sum
-    for k in range(hops):
-        summed = summed + moved(sent[hops + k], "blocks", k + 1).astype(F32)
-        summed = summed + moved(sent[hops - 1 - k], "blocks", -k - 1).astype(F32)
+    )(window, images, x_mat, x_twice, tap_lines, extra, odd)
+
+
+    def sent(value, step_of):
+        pairs = [(i, i + step_of(i)) for i in range(count) if 0 <= i + step_of(i) < count]
+        return lax.ppermute(value.astype(HALF), "blocks", pairs).astype(F32)
+
+    away = sent(far, lambda i: 3 if i % 2 else -3)
+    keep = keep + sent(mates, lambda i: -1 if i % 2 else 1)
+    summed = keep[1] + away + sent(keep[0], lambda i: -2) + sent(keep[2], lambda i: 2)
     return estimate * jnp.swapaxes(summed, 0, 1) / views
 
 

time: 154 us -> 134 us (0.87)
  waiting for transfers between devices: 33.6 us -> 25.4 us
  starting transfers between devices: 16.2 us -> 9.55 us
  Pallas kernels: 88.6 us -> 84.1 us
    pallas_call x1, Pallas kernels: 51.5 us -> 29 us  [body(): pl.pallas_call(functools.partial(window_kernel, count), out_shape=jax.Sha...]
    pallas_call x1, Pallas kernels: 37.1 us -> 55.1 us  [body(): pl.pallas_call(functools.partial(view_kernel, dims), out_shape=(jax.Shape...]
    ppermute x6 -> x4, waiting for transfers between devices: 33.6 us -> 25.4 us  [sent(): return lax.ppermute(value.astype(HALF), 'blocks', pairs).astype(F32)]
    ppermute x6 -> x4, starting transfers between devices: 16.2 us -> 9.55 us  [sent(): return lax.ppermute(value.astype(HALF), 'blocks', pairs).astype(F32)]
    convert_element_type x1 -> x2, other arithmetic: 3.2 us -> 2.32 us  [sent(): return lax.ppermute(value.astype(HALF), 'blocks', pairs).astype(F32)]
  transfers between devices with their start and end apart: 6 -> 4, of which waited for: 2 -> 3; matrix products, arithmetic and copies ran while one was open for 0% -> 1% of each run, Pallas kernels for 0% -> 0%
where the time goes in v2:
time: 134 us
  Pallas kernels  84.1 us (63%)
  waiting for transfers between devices  25.4 us (19%)
  starting transfers between devices  9.55 us (7%)
  other arithmetic  7.76 us (6%)
  local copies, waits for them, and re-layouts  6.63 us (5%)
    pallas_call x1, Pallas kernels, body(): pl.pallas_call(functools.partial(view_kernel, dims), out_shape=(jax.Shape...  55.1 us
    pallas_call x1, Pallas kernels, body(): pl.pallas_call(functools.partial(window_kernel, count), out_shape=jax.Sha...  29 us
    ppermute x4, waiting for transfers between devices, sent(): return lax.ppermute(value.astype(HALF), 'blocks', pairs).astype(F32)  25.4 us
    ppermute x4, starting transfers between devices, sent(): return lax.ppermute(value.astype(HALF), 'blocks', pairs).astype(F32)  9.55 us
  transfers between devices with their start and end apart: 4, of which 3 were waited for; matrix products, arithmetic and copies ran while one was open for 1% of the time, Pallas kernels for 0%

profile of v2, /device:TPU:0, one launch (start us, length us, event | category | flops | bytes accessed | tf_op | source)
XLA Modules:
  0.0 133.6 jit_solution(18292833002347946677)
XLA Ops:
  0.0 0.8 reduce_sum.29
  0.8 0.8 divide_convert_fusion
  1.6 0.7 sub.65
  2.5 0.7 add_add_fusion
  3.2 0.3 select_reduce_fusion
  3.8 0.5 and_select_fusion.extra_ref
  4.5 0.2 select_reduce_fusion.1
  4.7 0.6 copy.20.tap_ref
  5.3 0.7 copy.19.xm_ref
  6.1 0.6 pad_maximum_fusion.xt_ref
  6.7 2.6 %copy.27 = bf16[16,128,128]{2,0,1:T(8,128)(2,1)} copy(f32[16,128,128]{2,1,0:T(8,128)} %param.4) | data formatting | bytes 1572864 | tf_op args[0]
  9.3 29.0 %window.1.win_ref = bf16[7,128,16,128]{3,2,1,0:T(8,128)(2,1)} custom-call(bf16[128,16,128]{2,1,0:T(8,128)(2,1)} %bitcast.38), custom_call_target="tpu_custom_call" | custom-call | tf_op jit(solution)/shard_map/window/pallas_call | solution.py:229
  38.3 55.1 %views.1 = (f32[3,128,16,128]{3,2,1,0:T(8,128)}, f32[3,128,16,128]{3,2,1,0:T(8,128)}, f32[128,16,128]{2,1,0:T(8,128)}) custom-call(bf16[7,128,16,128]{3,2,1,0:T(8,128)(2,1)} %window.1.win_ref, bf16[8,16,128,128]{3,2,1,0:T(8,128)(2,1)} %img_ref.1, bf16[128,112]{1,0:T(8,128)(2,1)} %copy.19.xm_ref, bf16[112,256]{1,0:T(8,128)(2,1)} %pad_maximum_fusion.xt_ref, ...), custom_call_target="tpu_custom_call" | custom-call | tf_op jit(solution)/shard_map/views/pallas_call | solution.py:243
  93.4 2.2 %convert_element_type.61 = f16[3,128,16,128]{3,2,1,0:T(8,128)(2,1)S(1)} convert(f32[3,128,16,128]{3,2,1,0:T(8,128)} %get-tuple-element.9) | non-fusion elementwise | flops 786432 | bytes 4718592 | tf_op jit(solution)/shard_map/convert_element_type | solution.py:264
  95.8 0.7 collective-permute-start.1
  96.5 2.6 %collective-permute-done = f16[3,128,16,128]{3,2,1,0:T(8,128)(2,1)S(1)} collective-permute-done((f16[3,128,16,128]{3,2,1,0:T(8,128)(2,1)S(1)}, f16[3,128,16,128]{3,2,1,0:T(8,128)(2,1)S(1)}, u32[]{:S(2)}, u32[]{:S(2)}) %collective-permute-start) | collective-permute-done | bytes 1572896 | tf_op jit(solution)/shard_map/ppermute | solution.py:264
  99.1 0.5 fusion.9
  99.6 0.2 slice_bitcast_fusion.2
  99.9 1.4 %collective-permute-start.2 = (f16[128,16,128]{2,1,0:T(8,128)(2,1)S(1)}, f16[128,16,128]{2,1,0:T(8,128)(2,1)S(1)}, u32[]{:S(2)}, u32[]{:S(2)}) collective-permute-start(f16[128,16,128]{2,1,0:T(8,128)(2,1)S(1)} %get-tuple-element.13), channel_id=1, source_target_pairs={{2,0},{3,1},{4,2},{5,3},{6,4},{7,5},{8,6},{9,7},{10,8},{11,9},{12,... | collective-permute-start | bytes 1572872 | tf_op jit(solution)/shard_map/ppermute | solution.py:264
  101.3 7.4 %collective-permute-start.3 = (f16[128,16,128]{2,1,0:T(8,128)(2,1)S(1)}, f16[128,16,128]{2,1,0:T(8,128)(2,1)S(1)}, u32[]{:S(2)}, u32[]{:S(2)}) collective-permute-start(f16[128,16,128]{2,1,0:T(8,128)(2,1)S(1)} %get-tuple-element.14), channel_id=1, source_target_pairs={{0,2},{1,3},{2,4},{3,5},{4,6},{5,7},{6,8},{7,9},{8,10},{9,11},{10,... | collective-permute-start | bytes 1572872 | tf_op jit(solution)/shard_map/ppermute | solution.py:264
  108.7 10.5 %collective-permute-done.2 = f16[128,16,128]{2,1,0:T(8,128)(2,1)S(1)} collective-permute-done((f16[128,16,128]{2,1,0:T(8,128)(2,1)S(1)}, f16[128,16,128]{2,1,0:T(8,128)(2,1)S(1)}, u32[]{:S(2)}, u32[]{:S(2)}) %collective-permute-start.2) | collective-permute-done | bytes 524320 | tf_op jit(solution)/shard_map/ppermute | solution.py:264
  119.2 12.3 %collective-permute-done.3 = f16[128,16,128]{2,1,0:T(8,128)(2,1)S(1)} collective-permute-done((f16[128,16,128]{2,1,0:T(8,128)(2,1)S(1)}, f16[128,16,128]{2,1,0:T(8,128)(2,1)S(1)}, u32[]{:S(2)}, u32[]{:S(2)}) %collective-permute-start.3) | collective-permute-done | bytes 524320 | tf_op jit(solution)/shard_map/ppermute | solution.py:264
  131.5 0.8 fusion.5
  132.3 1.3 copy.22
  (26 shorter events, 0.7 us)
Async XLA Ops:
  93.4 2.3 %copy-start.2 = (f32[128,16,128]{2,1,0:T(8,128)S(1)}, f32[128,16,128]{2,1,0:T(8,128)}, u32[]{:S(2)}) copy-start(f32[128,16,128]{2,1,0:T(8,128)} %get-tuple-element.10) | copy-start | bytes 3145732
  93.4 5.7 %copy-start.1 = (f32[3,128,16,128]{3,2,1,0:T(8,128)S(1)}, f32[3,128,16,128]{3,2,1,0:T(8,128)}, u32[]{:S(2)}) copy-start(f32[3,128,16,128]{3,2,1,0:T(8,128)} %get-tuple-element.8) | copy-start | bytes 9437188
  95.6 3.5 %collective-permute-start = (f16[3,128,16,128]{3,2,1,0:T(8,128)(2,1)S(1)}, f16[3,128,16,128]{3,2,1,0:T(8,128)(2,1)S(1)}, u32[]{:S(2)}, u32[]{:S(2)}) collective-permute-start(f16[3,128,16,128]{3,2,1,0:T(8,128)(2,1)S(1)} %convert_element_type.61), channel_id=1, source_target_pairs={{0,1},{1,0},{2,3},{3,2},{4,5},{5,4},{6,7},{7,6},{8,9},{9,8},{10,11... | collective-permute-start | bytes 4718600 | tf_op jit(solution)/shard_map/ppermute | solution.py:264
  95.8 12.8 %collective-permute-start.1 = (f16[128,16,128]{2,1,0:T(8,128)(2,1)S(1)}, f16[128,16,128]{2,1,0:T(8,128)(2,1)S(1)}, u32[]{:S(2)}, u32[]{:S(2)}) collective-permute-start(f16[128,16,128]{2,1,0:T(8,128)(2,1)S(1)} %convert_element_type.63), channel_id=1, source_target_pairs={{1,4},{3,6},{4,1},{5,8},{6,3},{7,10},{8,5},{9,12},{10,7},{11,14},{... | collective-permute-start | bytes 1572872 | tf_op jit(solution)/shard_map/ppermute | solution.py:264
  99.6 31.9 %copy-start = (f32[16,128,128]{2,1,0:T(8,128)S(1)}, f32[16,128,128]{2,1,0:T(8,128)}, u32[]{:S(2)}) copy-start(f32[16,128,128]{2,1,0:T(8,128)} %param.4) | copy-start | bytes 3145732
  99.9 19.3 %collective-permute-start.2 = (f16[128,16,128]{2,1,0:T(8,128)(2,1)S(1)}, f16[128,16,128]{2,1,0:T(8,128)(2,1)S(1)}, u32[]{:S(2)}, u32[]{:S(2)}) collective-permute-start(f16[128,16,128]{2,1,0:T(8,128)(2,1)S(1)} %get-tuple-element.13), channel_id=1, source_target_pairs={{2,0},{3,1},{4,2},{5,3},{6,4},{7,5},{8,6},{9,7},{10,8},{11,9},{12,... | collective-permute-start | bytes 1572872 | tf_op jit(solution)/shard_map/ppermute | solution.py:264
  101.3 30.2 %collective-permute-start.3 = (f16[128,16,128]{2,1,0:T(8,128)(2,1)S(1)}, f16[128,16,128]{2,1,0:T(8,128)(2,1)S(1)}, u32[]{:S(2)}, u32[]{:S(2)}) collective-permute-start(f16[128,16,128]{2,1,0:T(8,128)(2,1)S(1)} %get-tuple-element.14), channel_id=1, source_target_pairs={{0,2},{1,3},{2,4},{3,5},{4,6},{5,7},{6,8},{7,9},{8,10},{9,11},{10,... | collective-permute-start | bytes 1572872 | tf_op jit(solution)/shard_map/ppermute | solution.py:264

commit v3 on v2

--- a/solution.py
+++ b/solution.py
@@ -8,6 +8,7 @@
 from jax.sharding import PartitionSpec as P
 
 SHIFT = 32
+PARTS = 4
 F32 = jnp.float32
 BF16 = jnp.bfloat16
 HALF = jnp.float16
@@ -19,12 +20,15 @@
     odd = lax.rem(me, 2)
     mid = 3
 
-    def send(src, slot, there, sem):
+    part = own_ref.shape[0] // PARTS
+
+    def send(src, slot, there, sem, j):
+        span = pl.ds(j * part, part)
         return pltpu.make_async_remote_copy(
-            src_ref=src,
-            dst_ref=out_ref.at[slot],
-            send_sem=send_sem.at[sem],
-            recv_sem=recv_sem.at[slot],
+            src_ref=src.at[span],
+            dst_ref=out_ref.at[slot, span],
+            send_sem=send_sem.at[sem, j],
+            recv_sem=recv_sem.at[slot, j],
             device_id={"blocks": there},
             device_id_type=MESH,
         )
@@ -45,16 +49,30 @@
         peers = 1 + low.astype(jnp.int32) + high.astype(jnp.int32) + away.astype(jnp.int32)
         pl.semaphore_wait(barrier, peers)
 
-        down = send(own_ref, mid + 2, me - 2, 0)
-        up = send(own_ref, mid - 2, me + 2, 1)
-        long = send(own_ref, mid - far, me + far, 2)
-        near = send(own_ref, mid - mate, me + mate, 3)
-        pass_low = send(out_ref.at[mid - 2], mid - 2 - mate, me + mate, 4)
-        pass_high = send(out_ref.at[mid + 2], mid + 2 - mate, me + mate, 5)
-        pl.when(low)(down.start)
-        pl.when(high)(up.start)
-        pl.when(away)(long.start)
-        near.start()
+        def down(j):
+            return send(own_ref, mid + 2, me - 2, 0, j)
+
+        def up(j):
+            return send(own_ref, mid - 2, me + 2, 1, j)
+
+        def long(j):
+            return send(own_ref, mid - far, me + far, 2, j)
+
+        def near(j):
+            return send(own_ref, mid - mate, me + mate, 3, j)
+
+        def pass_low(j):
+            return send(out_ref.at[mid - 2], mid - 2 - mate, me + mate, 4, j)
+
+        def pass_high(j):
+            return send(out_ref.at[mid + 2], mid + 2 - mate, me + mate, 5, j)
+
+        for j in range(PARTS):
+            pl.when(low)(lambda: down(j).start())
+            pl.when(high)(lambda: up(j).start())
+            near(j).start()
+        for j in range(PARTS):
+            pl.when(away)(lambda: long(j).start())
 
         out_ref[mid] = own_ref[...]
         for offset in (-3, -2, -1, 1, 2, 3):
@@ -65,43 +83,46 @@
                 def _():
                     out_ref[mid + offset] = jnp.zeros(own_ref.shape, own_ref.dtype)
 
-        @pl.when(low)
-        def _():
-            up.wait_recv()
-            pass_low.start()
-
-        @pl.when(high)
-        def _():
-            down.wait_recv()
-            pass_high.start()
-
-        send(own_ref, mid + mate, me + mate, 3).wait_recv()
-
-        @pl.when(low)
-        def _():
-            send(own_ref, mid - 2 + mate, me + mate, 4).wait_recv()
-            pass_low.wait_send()
-            down.wait_send()
-
-        @pl.when(high)
-        def _():
-            send(own_ref, mid + 2 + mate, me + mate, 5).wait_recv()
-            pass_high.wait_send()
-            up.wait_send()
-
-        @pl.when(away)
-        def _():
-            send(own_ref, mid + far, me + far, 2).wait_recv()
-            long.wait_send()
-
-        near.wait_send()
+        for j in range(PARTS):
+
+            @pl.when(low)
+            def _():
+                up(j).wait_recv()
+                pass_low(j).start()
+
+            @pl.when(high)
+            def _():
+                down(j).wait_recv()
+                pass_high(j).start()
+
+        for j in range(PARTS):
+            send(own_ref, mid + mate, me + mate, 3, j).wait_recv()
+
+            @pl.when(low)
+            def _():
+                send(own_ref, mid - 2 + mate, me + mate, 4, j).wait_recv()
+                pass_low(j).wait_send()
+                down(j).wait_send()
+
+            @pl.when(high)
+            def _():
+                send(own_ref, mid + 2 + mate, me + mate, 5, j).wait_recv()
+                pass_high(j).wait_send()
+                up(j).wait_send()
+
+            @pl.when(away)
+            def _():
+                send(own_ref, mid + far, me + far, 2, j).wait_recv()
+                long(j).wait_send()
+
+            near(j).wait_send()
 
     pl.when(odd == 0)(lambda: run(1, -3))
     pl.when(odd == 1)(lambda: run(-1, 3))
 
 
 def view_kernel(
-    dims, win_ref, img_ref, xm_ref, xt_ref, tap_ref, extra_ref, odd_ref, keep_ref, mate_ref, far_ref, held, low, mats
+    dims, win_ref, img_ref, xm_ref, xt_ref, tap_ref, extra_ref, keep_ref, mate_ref, far_ref, held, low, mats
 ):
     views, rows, across, along, hops, margin = dims
     group = 16
@@ -166,19 +187,9 @@
             res = jnp.dot(xt_ref[...], stacked, preferred_element_type=F32)
             res = res.reshape(2 * hops + 1, rows, along)
             for k in range(3):
-                keep_ref[k, base + p] = res[2 * k + 1]
-
-            @pl.when(odd_ref[0] == 0)
-            def _():
-                for k in range(3):
-                    mate_ref[k, base + p] = res[2 * k + 2]
-                far_ref[base + p] = res[0]
-
-            @pl.when(odd_ref[0] == 1)
-            def _():
-                for k in range(3):
-                    mate_ref[k, base + p] = res[2 * k]
-                far_ref[base + p] = res[6]
+                keep_ref[k, base + p] = res[k]
+                mate_ref[k, base + p] = res[3 + k]
+            far_ref[base + p] = res[6]
 
 
 def vmem(n):
@@ -218,11 +229,11 @@
     )
     x_mat = jnp.where(valid[:, :, None], taken(kernel[:, 0][:, None, None, :], index), 0.0)
     x_mat = x_mat.astype(BF16).reshape(views * rows, width)
-    x_turned = x_mat.T
+    odd = lax.axis_index("blocks") % 2
+    order = jnp.where(odd == 1, jnp.array([1, 3, 5, 0, 2, 4, 6]), jnp.array([1, 3, 5, 2, 4, 6, 0]))
+    x_turned = x_mat.T.reshape(2 * hops + 1, rows, views * rows)[order].reshape(width, views * rows)
     x_twice = jnp.concatenate([x_turned, x_turned], axis=1)
     extra = jnp.where(valid, 0.0, 1.0).astype(F32).reshape(views * rows)
-
-    odd = lax.rem(lax.axis_index("blocks"), 2).astype(jnp.int32).reshape(1)
 
     block = (across, rows, along)
     mine = jnp.swapaxes(estimate.astype(BF16), 0, 1)
@@ -232,8 +243,8 @@
         in_specs=vmem(1),
         out_specs=vmem(1)[0],
         scratch_shapes=[
-            pltpu.SemaphoreType.DMA((2 * hops + 1,)),
-            pltpu.SemaphoreType.DMA((2 * hops + 1,)),
+            pltpu.SemaphoreType.DMA((6, PARTS)),
+            pltpu.SemaphoreType.DMA((2 * hops + 1, PARTS)),
         ],
         compiler_params=pltpu.CompilerParams(collective_id=0, has_side_effects=True),
         name="window",
@@ -247,7 +258,7 @@
             jax.ShapeDtypeStruct((3,) + block, F32),
             jax.ShapeDtypeStruct(block, F32),
         ),
-        in_specs=vmem(5) + [pl.BlockSpec(memory_space=pltpu.SMEM)] * 2,
+        in_specs=vmem(5) + [pl.BlockSpec(memory_space=pltpu.SMEM)],
         out_specs=tuple(vmem(3)),
         scratch_shapes=[
             pltpu.VMEM((views * rows, across, along), BF16),
@@ -256,7 +267,7 @@
         ],
         compiler_params=pltpu.CompilerParams(vmem_limit_bytes=56 * 1024 * 1024),
         name="views",
-    )(window, images, x_mat, x_twice, tap_lines, extra, odd)
+    )(window, images, x_mat, x_twice, tap_lines, extra)
 
 
     def sent(value, step_of):

time: 134 us -> 116 us (0.87)
  Pallas kernels: 84.1 us -> 66.5 us
    pallas_call x1, Pallas kernels: 55.1 us -> 37.1 us  [body(): pl.pallas_call(functools.partial(view_kernel, dims), out_shape=(jax.Shape...]
where the time goes in v3:
time: 116 us; the launch traced here: 115 us
  Pallas kernels  66.5 us (57%)
  waiting for transfers between devices  25.1 us (22%)
  other arithmetic  8.51 us (7%)
  starting transfers between devices  8.4 us (7%)
  local copies, waits for them, and re-layouts  6.51 us (6%)
    pallas_call x1, Pallas kernels, body(): pl.pallas_call(functools.partial(view_kernel, dims), out_shape=(jax.Shape...  37.1 us
    pallas_call x1, Pallas kernels, body(): pl.pallas_call(functools.partial(window_kernel, count), out_shape=jax.Sha...  29.3 us
    ppermute x4, waiting for transfers between devices, sent(): return lax.ppermute(value.astype(HALF), 'blocks', pairs).astype(F32)  25.1 us
    ppermute x4, starting transfers between devices, sent(): return lax.ppermute(value.astype(HALF), 'blocks', pairs).astype(F32)  8.4 us
    unnamed x9, local copies, waits for them, and re-layouts  2.65 us
    convert_element_type x2, other arithmetic, sent(): return lax.ppermute(value.astype(HALF), 'blocks', pairs).astype(F32)  2.32 us
  transfers between devices with their start and end apart: 4, of which 3 were waited for; matrix products, arithmetic and copies ran while one was open for 1% of the time, Pallas kernels for 0%

profile of v3, /device:TPU:0, one launch (start us, length us, event | category | flops | bytes accessed | tf_op | source)
XLA Modules:
  0.0 115.2 jit_solution(17801837887680724068)
XLA Ops:
  0.0 0.7 compare_select_fusion
  0.7 0.8 reduce_sum.29
  1.5 0.8 divide_convert_fusion
  2.3 0.7 sub.65
  3.3 0.6 and_select_fusion.extra_ref
  4.2 0.6 copy.19.tap_ref
  4.8 0.7 add_add_fusion
  5.5 0.3 select_reduce_fusion
  6.1 0.6 gather_fusion
  6.7 0.6 pad_maximum_fusion.xt_ref
  7.3 2.6 %copy.26 = bf16[16,128,128]{2,0,1:T(8,128)(2,1)} copy(f32[16,128,128]{2,1,0:T(8,128)} %param.6) | data formatting | bytes 1572864 | tf_op args[0]
  9.9 29.3 %window.1.win_ref = bf16[7,128,16,128]{3,2,1,0:T(8,128)(2,1)} custom-call(bf16[128,16,128]{2,1,0:T(8,128)(2,1)} %bitcast.41), custom_call_target="tpu_custom_call" | custom-call | tf_op jit(solution)/shard_map/window/pallas_call | solution.py:240
  39.2 37.1 %views.1 = (f32[3,128,16,128]{3,2,1,0:T(8,128)}, f32[3,128,16,128]{3,2,1,0:T(8,128)}, f32[128,16,128]{2,1,0:T(8,128)}) custom-call(bf16[7,128,16,128]{3,2,1,0:T(8,128)(2,1)} %window.1.win_ref, bf16[8,16,128,128]{3,2,1,0:T(8,128)(2,1)} %img_ref.1, bf16[128,112]{1,0:T(8,128)(2,1)} %copy-done.3, bf16[112,256]{1,0:T(8,128)(2,1)} %pad_maximum_fusion.xt_ref, ...), custom_call_target="tpu_custom_call" | custom-call | tf_op jit(solution)/shard_map/views/pallas_call | solution.py:254
  76.4 2.2 %convert_element_type.61 = f16[3,128,16,128]{3,2,1,0:T(8,128)(2,1)S(1)} convert(f32[3,128,16,128]{3,2,1,0:T(8,128)} %get-tuple-element.9) | non-fusion elementwise | flops 786432 | bytes 4718592 | tf_op jit(solution)/shard_map/convert_element_type | solution.py:275
  78.8 0.7 collective-permute-start.1
  79.5 2.6 %collective-permute-done = f16[3,128,16,128]{3,2,1,0:T(8,128)(2,1)S(1)} collective-permute-done((f16[3,128,16,128]{3,2,1,0:T(8,128)(2,1)S(1)}, f16[3,128,16,128]{3,2,1,0:T(8,128)(2,1)S(1)}, u32[]{:S(2)}, u32[]{:S(2)}) %collective-permute-start) | collective-permute-done | bytes 1572896 | tf_op jit(solution)/shard_map/ppermute | solution.py:275
  82.1 0.5 fusion.10
  82.6 0.2 slice_bitcast_fusion.2
  82.9 1.4 %collective-permute-start.2 = (f16[128,16,128]{2,1,0:T(8,128)(2,1)S(1)}, f16[128,16,128]{2,1,0:T(8,128)(2,1)S(1)}, u32[]{:S(2)}, u32[]{:S(2)}) collective-permute-start(f16[128,16,128]{2,1,0:T(8,128)(2,1)S(1)} %get-tuple-element.13), channel_id=1, source_target_pairs={{2,0},{3,1},{4,2},{5,3},{6,4},{7,5},{8,6},{9,7},{10,8},{11,9},{12,... | collective-permute-start | bytes 1572872 | tf_op jit(solution)/shard_map/ppermute | solution.py:275
  84.3 6.2 %collective-permute-start.3 = (f16[128,16,128]{2,1,0:T(8,128)(2,1)S(1)}, f16[128,16,128]{2,1,0:T(8,128)(2,1)S(1)}, u32[]{:S(2)}, u32[]{:S(2)}) collective-permute-start(f16[128,16,128]{2,1,0:T(8,128)(2,1)S(1)} %get-tuple-element.14), channel_id=1, source_target_pairs={{0,2},{1,3},{2,4},{3,5},{4,6},{5,7},{6,8},{7,9},{8,10},{9,11},{10,... | collective-permute-start | bytes 1572872 | tf_op jit(solution)/shard_map/ppermute | solution.py:275
  90.5 9.9 %collective-permute-done.2 = f16[128,16,128]{2,1,0:T(8,128)(2,1)S(1)} collective-permute-done((f16[128,16,128]{2,1,0:T(8,128)(2,1)S(1)}, f16[128,16,128]{2,1,0:T(8,128)(2,1)S(1)}, u32[]{:S(2)}, u32[]{:S(2)}) %collective-permute-start.2) | collective-permute-done | bytes 524320 | tf_op jit(solution)/shard_map/ppermute | solution.py:275
  100.4 12.6 %collective-permute-done.3 = f16[128,16,128]{2,1,0:T(8,128)(2,1)S(1)} collective-permute-done((f16[128,16,128]{2,1,0:T(8,128)(2,1)S(1)}, f16[128,16,128]{2,1,0:T(8,128)(2,1)S(1)}, u32[]{:S(2)}, u32[]{:S(2)}) %collective-permute-start.3) | collective-permute-done | bytes 524320 | tf_op jit(solution)/shard_map/ppermute | solution.py:275
  113.1 0.8 fusion.5
  113.9 1.3 %copy.21 = f32[16,128,128]{2,1,0:T(8,128)} copy(f32[16,128,128]{2,0,1:T(8,128)S(1)} %fusion.5) | data formatting | bytes 2097152 | tf_op jit(solution)/shard_map/div | solution.py:280
  (29 shorter events, 1.0 us)
Async XLA Ops:
  6.0 33.3 %copy-start.3 = (bf16[128,112]{1,0:T(8,128)(2,1)}, bf16[128,112]{1,0:T(8,128)(2,1)S(1)}, u32[]{:S(2)}) copy-start(bf16[128,112]{1,0:T(8,128)(2,1)S(1)} %fusion.7.xm_ref) | copy-start | bytes 86020
  76.4 2.3 %copy-start.2 = (f32[128,16,128]{2,1,0:T(8,128)S(1)}, f32[128,16,128]{2,1,0:T(8,128)}, u32[]{:S(2)}) copy-start(f32[128,16,128]{2,1,0:T(8,128)} %get-tuple-element.10) | copy-start | bytes 3145732
  76.4 5.7 %copy-start.1 = (f32[3,128,16,128]{3,2,1,0:T(8,128)S(1)}, f32[3,128,16,128]{3,2,1,0:T(8,128)}, u32[]{:S(2)}) copy-start(f32[3,128,16,128]{3,2,1,0:T(8,128)} %get-tuple-element.8) | copy-start | bytes 9437188
  78.6 3.5 %collective-permute-start = (f16[3,128,16,128]{3,2,1,0:T(8,128)(2,1)S(1)}, f16[3,128,16,128]{3,2,1,0:T(8,128)(2,1)S(1)}, u32[]{:S(2)}, u32[]{:S(2)}) collective-permute-start(f16[3,128,16,128]{3,2,1,0:T(8,128)(2,1)S(1)} %convert_element_type.61), channel_id=1, source_target_pairs={{0,1},{1,0},{2,3},{3,2},{4,5},{5,4},{6,7},{7,6},{8,9},{9,8},{10,11... | collective-permute-start | bytes 4718600 | tf_op jit(solution)/shard_map/ppermute | solution.py:275
  78.8 11.7 %collective-permute-start.1 = (f16[128,16,128]{2,1,0:T(8,128)(2,1)S(1)}, f16[128,16,128]{2,1,0:T(8,128)(2,1)S(1)}, u32[]{:S(2)}, u32[]{:S(2)}) collective-permute-start(f16[128,16,128]{2,1,0:T(8,128)(2,1)S(1)} %convert_element_type.63), channel_id=1, source_target_pairs={{1,4},{3,6},{4,1},{5,8},{6,3},{7,10},{8,5},{9,12},{10,7},{11,14},{... | collective-permute-start | bytes 1572872 | tf_op jit(solution)/shard_map/ppermute | solution.py:275
  82.6 30.4 %copy-start = (f32[16,128,128]{2,1,0:T(8,128)S(1)}, f32[16,128,128]{2,1,0:T(8,128)}, u32[]{:S(2)}) copy-start(f32[16,128,128]{2,1,0:T(8,128)} %param.6) | copy-start | bytes 3145732
  82.9 17.6 %collective-permute-start.2 = (f16[128,16,128]{2,1,0:T(8,128)(2,1)S(1)}, f16[128,16,128]{2,1,0:T(8,128)(2,1)S(1)}, u32[]{:S(2)}, u32[]{:S(2)}) collective-permute-start(f16[128,16,128]{2,1,0:T(8,128)(2,1)S(1)} %get-tuple-element.13), channel_id=1, source_target_pairs={{2,0},{3,1},{4,2},{5,3},{6,4},{7,5},{8,6},{9,7},{10,8},{11,9},{12,... | collective-permute-start | bytes 1572872 | tf_op jit(solution)/shard_map/ppermute | solution.py:275
  84.3 28.8 %collective-permute-start.3 = (f16[128,16,128]{2,1,0:T(8,128)(2,1)S(1)}, f16[128,16,128]{2,1,0:T(8,128)(2,1)S(1)}, u32[]{:S(2)}, u32[]{:S(2)}) collective-permute-start(f16[128,16,128]{2,1,0:T(8,128)(2,1)S(1)} %get-tuple-element.14), channel_id=1, source_target_pairs={{0,2},{1,3},{2,4},{3,5},{4,6},{5,7},{6,8},{7,9},{8,10},{9,11},{10,... | collective-permute-start | bytes 1572872 | tf_op jit(solution)/shard_map/ppermute | solution.py:275

commit v4 on v3

--- a/solution.py
+++ b/solution.py
@@ -18,6 +18,7 @@
 def window_kernel(count, own_ref, out_ref, send_sem, recv_sem):
     me = lax.axis_index("blocks")
     odd = lax.rem(me, 2)
+    right = lax.rem(me, 4) >= 2
     mid = 3
 
     part = own_ref.shape[0] // PARTS
@@ -33,9 +34,9 @@
             device_id_type=MESH,
         )
 
-    def run(mate, far):
-        low = me >= 2
-        high = me + 2 < count
+    def run(mate, far, side):
+        beyond = (me + 2 * side >= 0) & (me + 2 * side < count)
+        before = (me - 2 * side >= 0) & (me - 2 * side < count)
         away = (me + far >= 0) & (me + far < count)
         barrier = pltpu.get_barrier_semaphore()
 
@@ -43,17 +44,18 @@
             pl.semaphore_signal(barrier, inc=1, device_id={"blocks": there}, device_id_type=MESH)
 
         signal(me + mate)
-        pl.when(low)(lambda: signal(me - 2))
-        pl.when(high)(lambda: signal(me + 2))
+        signal(me + side)
+        pl.when(beyond)(lambda: signal(me + 2 * side))
+        pl.when(before)(lambda: signal(me - 2 * side))
         pl.when(away)(lambda: signal(me + far))
-        peers = 1 + low.astype(jnp.int32) + high.astype(jnp.int32) + away.astype(jnp.int32)
+        peers = 2 + beyond.astype(jnp.int32) + before.astype(jnp.int32) + away.astype(jnp.int32)
         pl.semaphore_wait(barrier, peers)
 
-        def down(j):
-            return send(own_ref, mid + 2, me - 2, 0, j)
-
-        def up(j):
-            return send(own_ref, mid - 2, me + 2, 1, j)
+        def direct(j):
+            return send(own_ref, mid - side, me + side, 0, j)
+
+        def onward(j):
+            return send(out_ref.at[mid + side], mid - side, me + 2 * side, 1, j)
 
         def long(j):
             return send(own_ref, mid - far, me + far, 2, j)
@@ -61,22 +63,24 @@
         def near(j):
             return send(own_ref, mid - mate, me + mate, 3, j)
 
-        def pass_low(j):
-            return send(out_ref.at[mid - 2], mid - 2 - mate, me + mate, 4, j)
-
-        def pass_high(j):
-            return send(out_ref.at[mid + 2], mid + 2 - mate, me + mate, 5, j)
-
-        for j in range(PARTS):
-            pl.when(low)(lambda: down(j).start())
-            pl.when(high)(lambda: up(j).start())
+        def pass_near(j):
+            return send(out_ref.at[mid + side], mid + side - mate, me + mate, 4, j)
+
+        def pass_back(j):
+            return send(out_ref.at[mid - side], mid - side - mate, me + mate, 5, j)
+
+        def landed(offset, j):
+            return send(own_ref, mid + offset, me + mate, 0, j)
+
+        for j in range(PARTS):
+            direct(j).start()
             near(j).start()
         for j in range(PARTS):
             pl.when(away)(lambda: long(j).start())
 
         out_ref[mid] = own_ref[...]
         for offset in (-3, -2, -1, 1, 2, 3):
-            if offset != mate:
+            if offset not in (mate, side):
                 there = me + offset
 
                 @pl.when((there < 0) | (there >= count))
@@ -84,41 +88,42 @@
                     out_ref[mid + offset] = jnp.zeros(own_ref.shape, own_ref.dtype)
 
         for j in range(PARTS):
-
-            @pl.when(low)
+            landed(side, j).wait_recv()
+            pl.when(beyond)(lambda: onward(j).start())
+            pass_near(j).start()
+        for j in range(PARTS):
+
+            @pl.when(before)
             def _():
-                up(j).wait_recv()
-                pass_low(j).start()
-
-            @pl.when(high)
+                landed(-side, j).wait_recv()
+                pass_back(j).start()
+
+        for j in range(PARTS):
+            landed(mate, j).wait_recv()
+            landed(side + mate, j).wait_recv()
+
+            @pl.when(before)
             def _():
-                down(j).wait_recv()
-                pass_high(j).start()
-
-        for j in range(PARTS):
-            send(own_ref, mid + mate, me + mate, 3, j).wait_recv()
-
-            @pl.when(low)
+                landed(mate - side, j).wait_recv()
+                pass_back(j).wait_send()
+
+            @pl.when(beyond)
             def _():
-                send(own_ref, mid - 2 + mate, me + mate, 4, j).wait_recv()
-                pass_low(j).wait_send()
-                down(j).wait_send()
-
-            @pl.when(high)
-            def _():
-                send(own_ref, mid + 2 + mate, me + mate, 5, j).wait_recv()
-                pass_high(j).wait_send()
-                up(j).wait_send()
+                onward(j).wait_send()
 
             @pl.when(away)
             def _():
-                send(own_ref, mid + far, me + far, 2, j).wait_recv()
+                landed(far, j).wait_recv()
                 long(j).wait_send()
 
+            pass_near(j).wait_send()
+            direct(j).wait_send()
             near(j).wait_send()
 
-    pl.when(odd == 0)(lambda: run(1, -3))
-    pl.when(odd == 1)(lambda: run(-1, 3))
+    for mate, far in ((1, -3), (-1, 3)):
+        for side in (2, -2):
+            here = (odd == (0 if mate == 1 else 1)) & ((right if side < 0 else jnp.logical_not(right)))
+            pl.when(here)(functools.partial(run, mate, far, side))
 
 
 def view_kernel(
@@ -141,12 +146,15 @@
     def _(g):
         base = pl.multiple_of(g * group, group)
         slabs = []
-        for p in range(group):
-            piece = win_ref[:, base + p].reshape(win_ref.shape[0] * rows, along)
-            slabs.append(jnp.dot(xm_ref[...], piece, preferred_element_type=F32).astype(BF16))
+        for p in range(0, group, 2):
+            pair = [win_ref[:, base + p + q].reshape(-1, along) for q in range(2)]
+            res = jnp.dot(
+                xm_ref[...], jnp.concatenate(pair, axis=1), preferred_element_type=F32
+            ).astype(BF16)
+            slabs += [res[:, :along], res[:, along:]]
         held[:, pl.ds(base, group), :] = jnp.swapaxes(jnp.stack(slabs), 0, 1)
 
-    some = 4
+    some = 8
     per = rows // some
 
     def both(left, block):
@@ -182,14 +190,17 @@
         base = pl.multiple_of(g * group, group)
         tops = jnp.swapaxes(held[:, pl.ds(base, group), :], 0, 1)
         lows = jnp.swapaxes(low[:, pl.ds(base, group), :], 0, 1)
-        for p in range(group):
-            stacked = jnp.concatenate([tops[p], lows[p]], axis=0)
-            res = jnp.dot(xt_ref[...], stacked, preferred_element_type=F32)
-            res = res.reshape(2 * hops + 1, rows, along)
-            for k in range(3):
-                keep_ref[k, base + p] = res[k]
-                mate_ref[k, base + p] = res[3 + k]
-            far_ref[base + p] = res[6]
+        for p in range(0, group, 2):
+            pair = [jnp.concatenate([tops[p + q], lows[p + q]], axis=0) for q in range(2)]
+            both_p = jnp.dot(
+                xt_ref[...], jnp.concatenate(pair, axis=1), preferred_element_type=F32
+            )
+            for q in range(2):
+                res = both_p[:, q * along : (q + 1) * along].reshape(7, rows, along)
+                for k in range(3):
+                    keep_ref[k, base + p + q] = res[k]
+                    mate_ref[k, base + p + q] = res[3 + k]
+                far_ref[base + p + q] = res[6]
 
 
 def vmem(n):

time: 116 us -> 101 us (0.87)
  Pallas kernels: 66.5 us -> 50.6 us
  starting transfers between devices: 8.4 us -> 9.83 us
    pallas_call x1, Pallas kernels: 37.1 us -> 26.8 us  [body(): pl.pallas_call(functools.partial(view_kernel, dims), out_shape=(jax.Shape...]
    pallas_call x1, Pallas kernels: 29.3 us -> 23.7 us  [body(): pl.pallas_call(functools.partial(window_kernel, count), out_shape=jax.Sha...]
    ppermute x4, starting transfers between devices: 8.4 us -> 9.83 us  [sent(): return lax.ppermute(value.astype(HALF), 'blocks', pairs).astype(F32)]
where the time goes in v4:
time: 101 us; the launch traced here: 100 us
  Pallas kernels  50.6 us (50%)
  waiting for transfers between devices  24.8 us (25%)
  starting transfers between devices  9.83 us (10%)
  other arithmetic  8.51 us (8%)
  local copies, waits for them, and re-layouts  6.51 us (6%)
    pallas_call x1, Pallas kernels, body(): pl.pallas_call(functools.partial(view_kernel, dims), out_shape=(jax.Shape...  26.8 us
    ppermute x4, waiting for transfers between devices, sent(): return lax.ppermute(value.astype(HALF), 'blocks', pairs).astype(F32)  24.8 us
    pallas_call x1, Pallas kernels, body(): pl.pallas_call(functools.partial(window_kernel, count), out_shape=jax.Sha...  23.7 us
    ppermute x4, starting transfers between devices, sent(): return lax.ppermute(value.astype(HALF), 'blocks', pairs).astype(F32)  9.83 us
    unnamed x9, local copies, waits for them, and re-layouts  2.65 us
    convert_element_type x2, other arithmetic, sent(): return lax.ppermute(value.astype(HALF), 'blocks', pairs).astype(F32)  2.32 us
  transfers between devices with their start and end apart: 4, of which 3 were waited for; matrix products, arithmetic and copies ran while one was open for 1% of the time, Pallas kernels for 0%

profile of v4, /device:TPU:0, one launch (start us, length us, event | category | flops | bytes accessed | tf_op | source)
XLA Modules:
  0.0 100.4 jit_solution(14530330319139289758)
XLA Ops:
  0.0 0.7 compare_select_fusion
  0.7 0.8 reduce_sum.29
  1.5 0.8 divide_convert_fusion
  2.3 0.7 sub.65
  3.3 0.6 and_select_fusion.extra_ref
  4.2 0.6 copy.19.tap_ref
  4.8 0.7 add_add_fusion
  5.5 0.3 select_reduce_fusion
  6.1 0.6 gather_fusion
  6.7 0.6 pad_maximum_fusion.xt_ref
  7.3 2.6 %copy.26 = bf16[16,128,128]{2,0,1:T(8,128)(2,1)} copy(f32[16,128,128]{2,1,0:T(8,128)} %param.6) | data formatting | bytes 1572864 | tf_op args[0]
  9.9 23.7 %window.1.win_ref = bf16[7,128,16,128]{3,2,1,0:T(8,128)(2,1)} custom-call(bf16[128,16,128]{2,1,0:T(8,128)(2,1)} %bitcast.41), custom_call_target="tpu_custom_call" | custom-call | tf_op jit(solution)/shard_map/window/pallas_call | solution.py:251
  33.7 26.8 %views.1 = (f32[3,128,16,128]{3,2,1,0:T(8,128)}, f32[3,128,16,128]{3,2,1,0:T(8,128)}, f32[128,16,128]{2,1,0:T(8,128)}) custom-call(bf16[7,128,16,128]{3,2,1,0:T(8,128)(2,1)} %window.1.win_ref, bf16[8,16,128,128]{3,2,1,0:T(8,128)(2,1)} %img_ref.1, bf16[128,112]{1,0:T(8,128)(2,1)} %copy-done.3, bf16[112,256]{1,0:T(8,128)(2,1)} %pad_maximum_fusion.xt_ref, ...), custom_call_target="tpu_custom_call" | custom-call | tf_op jit(solution)/shard_map/views/pallas_call | solution.py:265
  60.5 2.2 %convert_element_type.61 = f16[3,128,16,128]{3,2,1,0:T(8,128)(2,1)S(1)} convert(f32[3,128,16,128]{3,2,1,0:T(8,128)} %get-tuple-element.9) | non-fusion elementwise | flops 786432 | bytes 4718592 | tf_op jit(solution)/shard_map/convert_element_type | solution.py:286
  62.9 0.7 collective-permute-start.1
  63.6 2.6 %collective-permute-done = f16[3,128,16,128]{3,2,1,0:T(8,128)(2,1)S(1)} collective-permute-done((f16[3,128,16,128]{3,2,1,0:T(8,128)(2,1)S(1)}, f16[3,128,16,128]{3,2,1,0:T(8,128)(2,1)S(1)}, u32[]{:S(2)}, u32[]{:S(2)}) %collective-permute-start) | collective-permute-done | bytes 1572896 | tf_op jit(solution)/shard_map/ppermute | solution.py:286
  66.3 0.5 fusion.10
  66.8 0.2 slice_bitcast_fusion.2
  67.0 1.4 %collective-permute-start.2 = (f16[128,16,128]{2,1,0:T(8,128)(2,1)S(1)}, f16[128,16,128]{2,1,0:T(8,128)(2,1)S(1)}, u32[]{:S(2)}, u32[]{:S(2)}) collective-permute-start(f16[128,16,128]{2,1,0:T(8,128)(2,1)S(1)} %get-tuple-element.13), channel_id=1, source_target_pairs={{2,0},{3,1},{4,2},{5,3},{6,4},{7,5},{8,6},{9,7},{10,8},{11,9},{12,... | collective-permute-start | bytes 1572872 | tf_op jit(solution)/shard_map/ppermute | solution.py:286
  68.4 7.6 %collective-permute-start.3 = (f16[128,16,128]{2,1,0:T(8,128)(2,1)S(1)}, f16[128,16,128]{2,1,0:T(8,128)(2,1)S(1)}, u32[]{:S(2)}, u32[]{:S(2)}) collective-permute-start(f16[128,16,128]{2,1,0:T(8,128)(2,1)S(1)} %get-tuple-element.14), channel_id=1, source_target_pairs={{0,2},{1,3},{2,4},{3,5},{4,6},{5,7},{6,8},{7,9},{8,10},{9,11},{10,... | collective-permute-start | bytes 1572872 | tf_op jit(solution)/shard_map/ppermute | solution.py:286
  76.1 10.8 %collective-permute-done.2 = f16[128,16,128]{2,1,0:T(8,128)(2,1)S(1)} collective-permute-done((f16[128,16,128]{2,1,0:T(8,128)(2,1)S(1)}, f16[128,16,128]{2,1,0:T(8,128)(2,1)S(1)}, u32[]{:S(2)}, u32[]{:S(2)}) %collective-permute-start.2) | collective-permute-done | bytes 524320 | tf_op jit(solution)/shard_map/ppermute | solution.py:286
  86.8 11.4 %collective-permute-done.3 = f16[128,16,128]{2,1,0:T(8,128)(2,1)S(1)} collective-permute-done((f16[128,16,128]{2,1,0:T(8,128)(2,1)S(1)}, f16[128,16,128]{2,1,0:T(8,128)(2,1)S(1)}, u32[]{:S(2)}, u32[]{:S(2)}) %collective-permute-start.3) | collective-permute-done | bytes 524320 | tf_op jit(solution)/shard_map/ppermute | solution.py:286
  98.2 0.8 fusion.5
  99.1 1.3 %copy.21 = f32[16,128,128]{2,1,0:T(8,128)} copy(f32[16,128,128]{2,0,1:T(8,128)S(1)} %fusion.5) | data formatting | bytes 2097152 | tf_op jit(solution)/shard_map/div | solution.py:291
  (29 shorter events, 1.0 us)
Async XLA Ops:
  6.0 27.7 %copy-start.3 = (bf16[128,112]{1,0:T(8,128)(2,1)}, bf16[128,112]{1,0:T(8,128)(2,1)S(1)}, u32[]{:S(2)}) copy-start(bf16[128,112]{1,0:T(8,128)(2,1)S(1)} %fusion.7.xm_ref) | copy-start | bytes 86020
  60.5 2.3 %copy-start.2 = (f32[128,16,128]{2,1,0:T(8,128)S(1)}, f32[128,16,128]{2,1,0:T(8,128)}, u32[]{:S(2)}) copy-start(f32[128,16,128]{2,1,0:T(8,128)} %get-tuple-element.10) | copy-start | bytes 3145732
  60.5 5.7 %copy-start.1 = (f32[3,128,16,128]{3,2,1,0:T(8,128)S(1)}, f32[3,128,16,128]{3,2,1,0:T(8,128)}, u32[]{:S(2)}) copy-start(f32[3,128,16,128]{3,2,1,0:T(8,128)} %get-tuple-element.8) | copy-start | bytes 9437188
  62.8 3.5 %collective-permute-start = (f16[3,128,16,128]{3,2,1,0:T(8,128)(2,1)S(1)}, f16[3,128,16,128]{3,2,1,0:T(8,128)(2,1)S(1)}, u32[]{:S(2)}, u32[]{:S(2)}) collective-permute-start(f16[3,128,16,128]{3,2,1,0:T(8,128)(2,1)S(1)} %convert_element_type.61), channel_id=1, source_target_pairs={{0,1},{1,0},{2,3},{3,2},{4,5},{5,4},{6,7},{7,6},{8,9},{9,8},{10,11... | collective-permute-start | bytes 4718600 | tf_op jit(solution)/shard_map/ppermute | solution.py:286
  62.9 13.1 %collective-permute-start.1 = (f16[128,16,128]{2,1,0:T(8,128)(2,1)S(1)}, f16[128,16,128]{2,1,0:T(8,128)(2,1)S(1)}, u32[]{:S(2)}, u32[]{:S(2)}) collective-permute-start(f16[128,16,128]{2,1,0:T(8,128)(2,1)S(1)} %convert_element_type.63), channel_id=1, source_target_pairs={{1,4},{3,6},{4,1},{5,8},{6,3},{7,10},{8,5},{9,12},{10,7},{11,14},{... | collective-permute-start | bytes 1572872 | tf_op jit(solution)/shard_map/ppermute | solution.py:286
  66.8 31.5 %copy-start = (f32[16,128,128]{2,1,0:T(8,128)S(1)}, f32[16,128,128]{2,1,0:T(8,128)}, u32[]{:S(2)}) copy-start(f32[16,128,128]{2,1,0:T(8,128)} %param.6) | copy-start | bytes 3145732
  67.0 19.9 %collective-permute-start.2 = (f16[128,16,128]{2,1,0:T(8,128)(2,1)S(1)}, f16[128,16,128]{2,1,0:T(8,128)(2,1)S(1)}, u32[]{:S(2)}, u32[]{:S(2)}) collective-permute-start(f16[128,16,128]{2,1,0:T(8,128)(2,1)S(1)} %get-tuple-element.13), channel_id=1, source_target_pairs={{2,0},{3,1},{4,2},{5,3},{6,4},{7,5},{8,6},{9,7},{10,8},{11,9},{12,... | collective-permute-start | bytes 1572872 | tf_op jit(solution)/shard_map/ppermute | solution.py:286
  68.4 29.8 %collective-permute-start.3 = (f16[128,16,128]{2,1,0:T(8,128)(2,1)S(1)}, f16[128,16,128]{2,1,0:T(8,128)(2,1)S(1)}, u32[]{:S(2)}, u32[]{:S(2)}) collective-permute-start(f16[128,16,128]{2,1,0:T(8,128)(2,1)S(1)} %get-tuple-element.14), channel_id=1, source_target_pairs={{0,2},{1,3},{2,4},{3,5},{4,6},{5,7},{6,8},{7,9},{8,10},{9,11},{10,... | collective-permute-start | bytes 1572872 | tf_op jit(solution)/shard_map/ppermute | solution.py:286

commit v5 on v4

--- a/solution.py
+++ b/solution.py
@@ -8,7 +8,7 @@
 from jax.sharding import PartitionSpec as P
 
 SHIFT = 32
-PARTS = 4
+PARTS = 8
 F32 = jnp.float32
 BF16 = jnp.bfloat16
 HALF = jnp.float16
@@ -74,9 +74,8 @@
 
         for j in range(PARTS):
             direct(j).start()
+            pl.when(away)(lambda: long(j).start())
             near(j).start()
-        for j in range(PARTS):
-            pl.when(away)(lambda: long(j).start())
 
         out_ref[mid] = own_ref[...]
         for offset in (-3, -2, -1, 1, 2, 3):
@@ -154,7 +153,7 @@
             slabs += [res[:, :along], res[:, along:]]
         held[:, pl.ds(base, group), :] = jnp.swapaxes(jnp.stack(slabs), 0, 1)
 
-    some = 8
+    some = 16
     per = rows // some
 
     def both(left, block):

time: 101 us -> 96.6 us (0.956)
  Pallas kernels: 50.6 us -> 45.8 us
    pallas_call x1, Pallas kernels: 26.8 us -> 22.3 us  [body(): pl.pallas_call(functools.partial(view_kernel, dims), out_shape=(jax.Shape...]
where the time goes in v5:
time: 96.6 us; the launch traced here: 96.2 us
  Pallas kernels  45.8 us (47%)
  waiting for transfers between devices  24.4 us (25%)
  starting transfers between devices  10.8 us (11%)
  other arithmetic  8.51 us (9%)
  local copies, waits for them, and re-layouts  6.51 us (7%)
    ppermute x4, waiting for transfers between devices, sent(): return lax.ppermute(value.astype(HALF), 'blocks', pairs).astype(F32)  24.4 us
    pallas_call x1, Pallas kernels, body(): pl.pallas_call(functools.partial(window_kernel, count), out_shape=jax.Sha...  23.6 us
    pallas_call x1, Pallas kernels, body(): pl.pallas_call(functools.partial(view_kernel, dims), out_shape=(jax.Shape...  22.3 us
    ppermute x4, starting transfers between devices, sent(): return lax.ppermute(value.astype(HALF), 'blocks', pairs).astype(F32)  10.8 us
    unnamed x9, local copies, waits for them, and re-layouts  2.65 us
    convert_element_type x2, other arithmetic, sent(): return lax.ppermute(value.astype(HALF), 'blocks', pairs).astype(F32)  2.32 us
  transfers between devices with their start and end apart: 4, of which 3 were waited for; matrix products, arithmetic and copies ran while one was open for 1% of the time, Pallas kernels for 0%

profile of v5, /device:TPU:0, one launch (start us, length us, event | category | flops | bytes accessed | tf_op | source)
XLA Modules:
  0.0 96.2 jit_solution(11998147602256008001)
XLA Ops:
  0.0 0.7 compare_select_fusion
  0.7 0.8 reduce_sum.29
  1.5 0.8 divide_convert_fusion
  2.3 0.7 sub.65
  3.3 0.6 and_select_fusion.extra_ref
  4.2 0.6 copy.19.tap_ref
  4.8 0.7 add_add_fusion
  5.5 0.3 select_reduce_fusion
  6.1 0.6 gather_fusion
  6.7 0.6 pad_maximum_fusion.xt_ref
  7.3 2.6 %copy.26 = bf16[16,128,128]{2,0,1:T(8,128)(2,1)} copy(f32[16,128,128]{2,1,0:T(8,128)} %param.6) | data formatting | bytes 1572864 | tf_op args[0]
  9.9 23.6 %window.1.win_ref = bf16[7,128,16,128]{3,2,1,0:T(8,128)(2,1)} custom-call(bf16[128,16,128]{2,1,0:T(8,128)(2,1)} %bitcast.41), custom_call_target="tpu_custom_call" | custom-call | tf_op jit(solution)/shard_map/window/pallas_call | solution.py:250
  33.5 22.3 %views.1 = (f32[3,128,16,128]{3,2,1,0:T(8,128)}, f32[3,128,16,128]{3,2,1,0:T(8,128)}, f32[128,16,128]{2,1,0:T(8,128)}) custom-call(bf16[7,128,16,128]{3,2,1,0:T(8,128)(2,1)} %window.1.win_ref, bf16[8,16,128,128]{3,2,1,0:T(8,128)(2,1)} %img_ref.1, bf16[128,112]{1,0:T(8,128)(2,1)} %copy-done.3, bf16[112,256]{1,0:T(8,128)(2,1)} %pad_maximum_fusion.xt_ref, ...), custom_call_target="tpu_custom_call" | custom-call | tf_op jit(solution)/shard_map/views/pallas_call | solution.py:264
  55.8 2.2 %convert_element_type.61 = f16[3,128,16,128]{3,2,1,0:T(8,128)(2,1)S(1)} convert(f32[3,128,16,128]{3,2,1,0:T(8,128)} %get-tuple-element.9) | non-fusion elementwise | flops 786432 | bytes 4718592 | tf_op jit(solution)/shard_map/convert_element_type | solution.py:285
  58.0 0.8 collective-permute-start
  58.9 0.7 collective-permute-start.1
  59.6 2.3 %collective-permute-done = f16[3,128,16,128]{3,2,1,0:T(8,128)(2,1)S(1)} collective-permute-done((f16[3,128,16,128]{3,2,1,0:T(8,128)(2,1)S(1)}, f16[3,128,16,128]{3,2,1,0:T(8,128)(2,1)S(1)}, u32[]{:S(2)}, u32[]{:S(2)}) %collective-permute-start) | collective-permute-done | bytes 1572896 | tf_op jit(solution)/shard_map/ppermute | solution.py:285
  61.9 0.5 fusion.10
  62.6 1.4 %collective-permute-start.2 = (f16[128,16,128]{2,1,0:T(8,128)(2,1)S(1)}, f16[128,16,128]{2,1,0:T(8,128)(2,1)S(1)}, u32[]{:S(2)}, u32[]{:S(2)}) collective-permute-start(f16[128,16,128]{2,1,0:T(8,128)(2,1)S(1)} %get-tuple-element.13), channel_id=1, source_target_pairs={{2,0},{3,1},{4,2},{5,3},{6,4},{7,5},{8,6},{9,7},{10,8},{11,9},{12,... | collective-permute-start | bytes 1572872 | tf_op jit(solution)/shard_map/ppermute | solution.py:285
  64.0 7.8 %collective-permute-start.3 = (f16[128,16,128]{2,1,0:T(8,128)(2,1)S(1)}, f16[128,16,128]{2,1,0:T(8,128)(2,1)S(1)}, u32[]{:S(2)}, u32[]{:S(2)}) collective-permute-start(f16[128,16,128]{2,1,0:T(8,128)(2,1)S(1)} %get-tuple-element.14), channel_id=1, source_target_pairs={{0,2},{1,3},{2,4},{3,5},{4,6},{5,7},{6,8},{7,9},{8,10},{9,11},{10,... | collective-permute-start | bytes 1572872 | tf_op jit(solution)/shard_map/ppermute | solution.py:285
  71.9 10.7 %collective-permute-done.2 = f16[128,16,128]{2,1,0:T(8,128)(2,1)S(1)} collective-permute-done((f16[128,16,128]{2,1,0:T(8,128)(2,1)S(1)}, f16[128,16,128]{2,1,0:T(8,128)(2,1)S(1)}, u32[]{:S(2)}, u32[]{:S(2)}) %collective-permute-start.2) | collective-permute-done | bytes 524320 | tf_op jit(solution)/shard_map/ppermute | solution.py:285
  82.6 11.4 %collective-permute-done.3 = f16[128,16,128]{2,1,0:T(8,128)(2,1)S(1)} collective-permute-done((f16[128,16,128]{2,1,0:T(8,128)(2,1)S(1)}, f16[128,16,128]{2,1,0:T(8,128)(2,1)S(1)}, u32[]{:S(2)}, u32[]{:S(2)}) %collective-permute-start.3) | collective-permute-done | bytes 524320 | tf_op jit(solution)/shard_map/ppermute | solution.py:285
  94.0 0.8 fusion.5
  94.9 1.3 %copy.21 = f32[16,128,128]{2,1,0:T(8,128)} copy(f32[16,128,128]{2,0,1:T(8,128)S(1)} %fusion.5) | data formatting | bytes 2097152 | tf_op jit(solution)/shard_map/div | solution.py:290
  (29 shorter events, 1.1 us)
Async XLA Ops:
  6.0 27.5 %copy-start.3 = (bf16[128,112]{1,0:T(8,128)(2,1)}, bf16[128,112]{1,0:T(8,128)(2,1)S(1)}, u32[]{:S(2)}) copy-start(bf16[128,112]{1,0:T(8,128)(2,1)S(1)} %fusion.7.xm_ref) | copy-start | bytes 86020
  55.8 3.1 %copy-start.2 = (f32[128,16,128]{2,1,0:T(8,128)S(1)}, f32[128,16,128]{2,1,0:T(8,128)}, u32[]{:S(2)}) copy-start(f32[128,16,128]{2,1,0:T(8,128)} %get-tuple-element.10) | copy-start | bytes 3145732
  55.8 6.1 %copy-start.1 = (f32[3,128,16,128]{3,2,1,0:T(8,128)S(1)}, f32[3,128,16,128]{3,2,1,0:T(8,128)}, u32[]{:S(2)}) copy-start(f32[3,128,16,128]{3,2,1,0:T(8,128)} %get-tuple-element.8) | copy-start | bytes 9437188
  58.0 3.9 %collective-permute-start = (f16[3,128,16,128]{3,2,1,0:T(8,128)(2,1)S(1)}, f16[3,128,16,128]{3,2,1,0:T(8,128)(2,1)S(1)}, u32[]{:S(2)}, u32[]{:S(2)}) collective-permute-start(f16[3,128,16,128]{3,2,1,0:T(8,128)(2,1)S(1)} %convert_element_type.61), channel_id=1, source_target_pairs={{0,1},{1,0},{2,3},{3,2},{4,5},{5,4},{6,7},{7,6},{8,9},{9,8},{10,11... | collective-permute-start | bytes 4718600 | tf_op jit(solution)/shard_map/ppermute | solution.py:285
  58.9 12.9 %collective-permute-start.1 = (f16[128,16,128]{2,1,0:T(8,128)(2,1)S(1)}, f16[128,16,128]{2,1,0:T(8,128)(2,1)S(1)}, u32[]{:S(2)}, u32[]{:S(2)}) collective-permute-start(f16[128,16,128]{2,1,0:T(8,128)(2,1)S(1)} %convert_element_type.63), channel_id=1, source_target_pairs={{1,4},{3,6},{4,1},{5,8},{6,3},{7,10},{8,5},{9,12},{10,7},{11,14},{... | collective-permute-start | bytes 1572872 | tf_op jit(solution)/shard_map/ppermute | solution.py:285
  62.4 31.6 %copy-start = (f32[16,128,128]{2,1,0:T(8,128)S(1)}, f32[16,128,128]{2,1,0:T(8,128)}, u32[]{:S(2)}) copy-start(f32[16,128,128]{2,1,0:T(8,128)} %param.6) | copy-start | bytes 3145732
  62.6 20.0 %collective-permute-start.2 = (f16[128,16,128]{2,1,0:T(8,128)(2,1)S(1)}, f16[128,16,128]{2,1,0:T(8,128)(2,1)S(1)}, u32[]{:S(2)}, u32[]{:S(2)}) collective-permute-start(f16[128,16,128]{2,1,0:T(8,128)(2,1)S(1)} %get-tuple-element.13), channel_id=1, source_target_pairs={{2,0},{3,1},{4,2},{5,3},{6,4},{7,5},{8,6},{9,7},{10,8},{11,9},{12,... | collective-permute-start | bytes 1572872 | tf_op jit(solution)/shard_map/ppermute | solution.py:285
  64.0 30.0 %collective-permute-start.3 = (f16[128,16,128]{2,1,0:T(8,128)(2,1)S(1)}, f16[128,16,128]{2,1,0:T(8,128)(2,1)S(1)}, u32[]{:S(2)}, u32[]{:S(2)}) collective-permute-start(f16[128,16,128]{2,1,0:T(8,128)(2,1)S(1)} %get-tuple-element.14), channel_id=1, source_target_pairs={{0,2},{1,3},{2,4},{3,5},{4,6},{5,7},{6,8},{7,9},{8,10},{9,11},{10,... | collective-permute-start | bytes 1572872 | tf_op jit(solution)/shard_map/ppermute | solution.py:285

commit v6 on v5

--- a/solution.py
+++ b/solution.py
@@ -129,7 +129,7 @@
     dims, win_ref, img_ref, xm_ref, xt_ref, tap_ref, extra_ref, keep_ref, mate_ref, far_ref, held, low, mats
 ):
     views, rows, across, along, hops, margin = dims
-    group = 16
+    group = 32
     r = lax.broadcasted_iota(jnp.int32, (along, along), 0)
     c = lax.broadcasted_iota(jnp.int32, (along, along), 1)
     near = jnp.abs(r - c) <= margin

time: 96.6 us -> 95.2 us (0.986)
  Pallas kernels: 45.8 us -> 44.5 us
    pallas_call x1, Pallas kernels: 22.3 us -> 20.9 us  [body(): pl.pallas_call(functools.partial(view_kernel, dims), out_shape=(jax.Shape...]
where the time goes in v6:
time: 95.2 us; the launch traced here: 94.8 us
  Pallas kernels  44.5 us (47%)
  waiting for transfers between devices  24.4 us (26%)
  starting transfers between devices  10.7 us (11%)
  other arithmetic  8.51 us (9%)
  local copies, waits for them, and re-layouts  6.51 us (7%)
    ppermute x4, waiting for transfers between devices, sent(): return lax.ppermute(value.astype(HALF), 'blocks', pairs).astype(F32)  24.4 us
    pallas_call x1, Pallas kernels, body(): pl.pallas_call(functools.partial(window_kernel, count), out_shape=jax.Sha...  23.6 us
    pallas_call x1, Pallas kernels, body(): pl.pallas_call(functools.partial(view_kernel, dims), out_shape=(jax.Shape...  20.9 us
    ppermute x4, starting transfers between devices, sent(): return lax.ppermute(value.astype(HALF), 'blocks', pairs).astype(F32)  10.7 us
    unnamed x9, local copies, waits for them, and re-layouts  2.65 us
    convert_element_type x2, other arithmetic, sent(): return lax.ppermute(value.astype(HALF), 'blocks', pairs).astype(F32)  2.32 us
  transfers between devices with their start and end apart: 4, of which 3 were waited for; matrix products, arithmetic and copies ran while one was open for 1% of the time, Pallas kernels for 0%

profile of v6, /device:TPU:0, one launch (start us, length us, event | category | flops | bytes accessed | tf_op | source)
XLA Modules:
  0.0 94.8 jit_solution(18141134875968492047)
XLA Ops:
  0.0 0.7 compare_select_fusion
  0.7 0.8 reduce_sum.29
  1.5 0.8 divide_convert_fusion
  2.3 0.7 sub.65
  3.3 0.6 and_select_fusion.extra_ref
  4.2 0.6 copy.19.tap_ref
  4.8 0.7 add_add_fusion
  5.5 0.3 select_reduce_fusion
  6.1 0.6 gather_fusion
  6.7 0.6 pad_maximum_fusion.xt_ref
  7.3 2.6 %copy.26 = bf16[16,128,128]{2,0,1:T(8,128)(2,1)} copy(f32[16,128,128]{2,1,0:T(8,128)} %param.6) | data formatting | bytes 1572864 | tf_op args[0]
  9.9 23.6 %window.1.win_ref = bf16[7,128,16,128]{3,2,1,0:T(8,128)(2,1)} custom-call(bf16[128,16,128]{2,1,0:T(8,128)(2,1)} %bitcast.41), custom_call_target="tpu_custom_call" | custom-call | tf_op jit(solution)/shard_map/window/pallas_call | solution.py:250
  33.5 20.9 %views.1 = (f32[3,128,16,128]{3,2,1,0:T(8,128)}, f32[3,128,16,128]{3,2,1,0:T(8,128)}, f32[128,16,128]{2,1,0:T(8,128)}) custom-call(bf16[7,128,16,128]{3,2,1,0:T(8,128)(2,1)} %window.1.win_ref, bf16[8,16,128,128]{3,2,1,0:T(8,128)(2,1)} %img_ref.1, bf16[128,112]{1,0:T(8,128)(2,1)} %copy-done.3, bf16[112,256]{1,0:T(8,128)(2,1)} %pad_maximum_fusion.xt_ref, ...), custom_call_target="tpu_custom_call" | custom-call | tf_op jit(solution)/shard_map/views/pallas_call | solution.py:264
  54.4 2.2 %convert_element_type.61 = f16[3,128,16,128]{3,2,1,0:T(8,128)(2,1)S(1)} convert(f32[3,128,16,128]{3,2,1,0:T(8,128)} %get-tuple-element.9) | non-fusion elementwise | flops 786432 | bytes 4718592 | tf_op jit(solution)/shard_map/convert_element_type | solution.py:285
  56.7 0.8 collective-permute-start
  57.5 0.7 collective-permute-start.1
  58.2 2.3 %collective-permute-done = f16[3,128,16,128]{3,2,1,0:T(8,128)(2,1)S(1)} collective-permute-done((f16[3,128,16,128]{3,2,1,0:T(8,128)(2,1)S(1)}, f16[3,128,16,128]{3,2,1,0:T(8,128)(2,1)S(1)}, u32[]{:S(2)}, u32[]{:S(2)}) %collective-permute-start) | collective-permute-done | bytes 1572896 | tf_op jit(solution)/shard_map/ppermute | solution.py:285
  60.5 0.5 fusion.10
  61.2 1.4 %collective-permute-start.2 = (f16[128,16,128]{2,1,0:T(8,128)(2,1)S(1)}, f16[128,16,128]{2,1,0:T(8,128)(2,1)S(1)}, u32[]{:S(2)}, u32[]{:S(2)}) collective-permute-start(f16[128,16,128]{2,1,0:T(8,128)(2,1)S(1)} %get-tuple-element.13), channel_id=1, source_target_pairs={{2,0},{3,1},{4,2},{5,3},{6,4},{7,5},{8,6},{9,7},{10,8},{11,9},{12,... | collective-permute-start | bytes 1572872 | tf_op jit(solution)/shard_map/ppermute | solution.py:285
  62.7 7.8 %collective-permute-start.3 = (f16[128,16,128]{2,1,0:T(8,128)(2,1)S(1)}, f16[128,16,128]{2,1,0:T(8,128)(2,1)S(1)}, u32[]{:S(2)}, u32[]{:S(2)}) collective-permute-start(f16[128,16,128]{2,1,0:T(8,128)(2,1)S(1)} %get-tuple-element.14), channel_id=1, source_target_pairs={{0,2},{1,3},{2,4},{3,5},{4,6},{5,7},{6,8},{7,9},{8,10},{9,11},{10,... | collective-permute-start | bytes 1572872 | tf_op jit(solution)/shard_map/ppermute | solution.py:285
  70.5 10.8 %collective-permute-done.2 = f16[128,16,128]{2,1,0:T(8,128)(2,1)S(1)} collective-permute-done((f16[128,16,128]{2,1,0:T(8,128)(2,1)S(1)}, f16[128,16,128]{2,1,0:T(8,128)(2,1)S(1)}, u32[]{:S(2)}, u32[]{:S(2)}) %collective-permute-start.2) | collective-permute-done | bytes 524320 | tf_op jit(solution)/shard_map/ppermute | solution.py:285
  81.3 11.4 %collective-permute-done.3 = f16[128,16,128]{2,1,0:T(8,128)(2,1)S(1)} collective-permute-done((f16[128,16,128]{2,1,0:T(8,128)(2,1)S(1)}, f16[128,16,128]{2,1,0:T(8,128)(2,1)S(1)}, u32[]{:S(2)}, u32[]{:S(2)}) %collective-permute-start.3) | collective-permute-done | bytes 524320 | tf_op jit(solution)/shard_map/ppermute | solution.py:285
  92.7 0.8 fusion.5
  93.5 1.3 %copy.21 = f32[16,128,128]{2,1,0:T(8,128)} copy(f32[16,128,128]{2,0,1:T(8,128)S(1)} %fusion.5) | data formatting | bytes 2097152 | tf_op jit(solution)/shard_map/div | solution.py:290
  (29 shorter events, 1.1 us)
Async XLA Ops:
  6.0 27.5 %copy-start.3 = (bf16[128,112]{1,0:T(8,128)(2,1)}, bf16[128,112]{1,0:T(8,128)(2,1)S(1)}, u32[]{:S(2)}) copy-start(bf16[128,112]{1,0:T(8,128)(2,1)S(1)} %fusion.7.xm_ref) | copy-start | bytes 86020
  54.4 3.1 %copy-start.2 = (f32[128,16,128]{2,1,0:T(8,128)S(1)}, f32[128,16,128]{2,1,0:T(8,128)}, u32[]{:S(2)}) copy-start(f32[128,16,128]{2,1,0:T(8,128)} %get-tuple-element.10) | copy-start | bytes 3145732
  54.4 6.1 %copy-start.1 = (f32[3,128,16,128]{3,2,1,0:T(8,128)S(1)}, f32[3,128,16,128]{3,2,1,0:T(8,128)}, u32[]{:S(2)}) copy-start(f32[3,128,16,128]{3,2,1,0:T(8,128)} %get-tuple-element.8) | copy-start | bytes 9437188
  56.7 3.8 %collective-permute-start = (f16[3,128,16,128]{3,2,1,0:T(8,128)(2,1)S(1)}, f16[3,128,16,128]{3,2,1,0:T(8,128)(2,1)S(1)}, u32[]{:S(2)}, u32[]{:S(2)}) collective-permute-start(f16[3,128,16,128]{3,2,1,0:T(8,128)(2,1)S(1)} %convert_element_type.61), channel_id=1, source_target_pairs={{0,1},{1,0},{2,3},{3,2},{4,5},{5,4},{6,7},{7,6},{8,9},{9,8},{10,11... | collective-permute-start | bytes 4718600 | tf_op jit(solution)/shard_map/ppermute | solution.py:285
  57.5 12.9 %collective-permute-start.1 = (f16[128,16,128]{2,1,0:T(8,128)(2,1)S(1)}, f16[128,16,128]{2,1,0:T(8,128)(2,1)S(1)}, u32[]{:S(2)}, u32[]{:S(2)}) collective-permute-start(f16[128,16,128]{2,1,0:T(8,128)(2,1)S(1)} %convert_element_type.63), channel_id=1, source_target_pairs={{1,4},{3,6},{4,1},{5,8},{6,3},{7,10},{8,5},{9,12},{10,7},{11,14},{... | collective-permute-start | bytes 1572872 | tf_op jit(solution)/shard_map/ppermute | solution.py:285
  61.0 31.7 %copy-start = (f32[16,128,128]{2,1,0:T(8,128)S(1)}, f32[16,128,128]{2,1,0:T(8,128)}, u32[]{:S(2)}) copy-start(f32[16,128,128]{2,1,0:T(8,128)} %param.6) | copy-start | bytes 3145732
  61.2 20.0 %collective-permute-start.2 = (f16[128,16,128]{2,1,0:T(8,128)(2,1)S(1)}, f16[128,16,128]{2,1,0:T(8,128)(2,1)S(1)}, u32[]{:S(2)}, u32[]{:S(2)}) collective-permute-start(f16[128,16,128]{2,1,0:T(8,128)(2,1)S(1)} %get-tuple-element.13), channel_id=1, source_target_pairs={{2,0},{3,1},{4,2},{5,3},{6,4},{7,5},{8,6},{9,7},{10,8},{11,9},{12,... | collective-permute-start | bytes 1572872 | tf_op jit(solution)/shard_map/ppermute | solution.py:285
  62.7 30.0 %collective-permute-start.3 = (f16[128,16,128]{2,1,0:T(8,128)(2,1)S(1)}, f16[128,16,128]{2,1,0:T(8,128)(2,1)S(1)}, u32[]{:S(2)}, u32[]{:S(2)}) collective-permute-start(f16[128,16,128]{2,1,0:T(8,128)(2,1)S(1)} %get-tuple-element.14), channel_id=1, source_target_pairs={{0,2},{1,3},{2,4},{3,5},{4,6},{5,7},{6,8},{7,9},{8,10},{9,11},{10,... | collective-permute-start | bytes 1572872 | tf_op jit(solution)/shard_map/ppermute | solution.py:285
